TPU v7x, 32 devices: a whole 2x2x4 slice. The times are simulated.
32 devices in a mesh: scene: 2 (over x), track: 16 (over z, y, core).
Axes of the slice: x: 2, y: 2, z: 4, core: 2. Of those that a mesh axis runs over, the one named last changes fastest.
Arguments:
- panels: bfloat16 [32, 16, 2, 16, 2048], P(('scene', 'track')), parts along dimension 0, may hold values from -6 to 6
- kernel: bfloat16 [3, 2, 2048, 512], replicated, may hold values from -0.09375 to 0.09375
- steering: float32 [2, 64, 16], replicated, may hold values from -1 to 1
- beam_strips: int32 [32, 3], P('scene'), parts along dimension 0, may hold values from -1 to 15, as said below
- range_blocks: int32 [32, 8], P('scene'), parts along dimension 0, may hold values from 0 to 15
Outputs:
- volume: float32 [2, 64, 16, 4096], P(None, None, 'scene', 'track'), parts along dimension 2
There are 2 independent parts, one for each index of `scene`. A program takes and returns all parts, laid end to end along the dimension named above; an argument that names none is the same for every part. Nothing has to cross between parts.
Inputs may be any that keep to these rules, and one draw needn't show every extreme that they name: `beam_strips`: row b lists the strips c - 1, c, c + 1 for a centre c = b + o with o in -1, 0, 1, each outside 0 .. 15 replaced by -1; block 0 has o <= 0.
All inputs are finite; a program needn't handle non-finite values.
Results may differ from a plain program's by a relative error of at most 0.003.
Values may be sent and summed in bfloat16 or wider, within the bound.
No kernel may reach another device: no remote copies, remote signals or barrier semaphores. Data moves between devices by JAX's collectives and lax.ppermute only.
A program may use at most 64 MiB of HBM per device.

v0:
```python
import functools

import jax
import jax.numpy as jnp
from jax import lax
from jax.experimental import pallas as pl
from jax.experimental.pallas import tpu as pltpu
from jax.sharding import PartitionSpec as P


F32 = jnp.float32
BF16 = jnp.bfloat16
VMEM_SPEC = pl.BlockSpec(memory_space=pltpu.VMEM)
HBM_SPEC = pl.BlockSpec(memory_space=pltpu.MemorySpace.HBM)


def backproject(
    strips_hbm, ranges_hbm, panel_hbm, kernel_hbm,
    swap_ref, mid_ref, far_ref, near_ref, own_ref, next_ref,
    strips_ref, ranges_ref, rows, taps, slots, table_sem, row_sem, tap_sem,
):
    block = lax.axis_index("track")
    beams, _, span, footprint = kernel_hbm.shape
    tiles = ranges_ref.shape[0]
    tracks = panel_hbm.shape[3]
    half = footprint // 4
    cols = footprint // 2
    tile_rows = 2 * tracks

    tables = [
        pltpu.make_async_copy(strips_hbm, strips_ref, table_sem.at[0]),
        pltpu.make_async_copy(ranges_hbm, ranges_ref, table_sem.at[1]),
    ]
    for copy in tables:
        copy.start()
    tap_copies = []
    for j in range(beams):
        for c in range(2):
            copy = pltpu.make_async_copy(
                kernel_hbm.at[j, :, :, c * cols : (c + 1) * cols], taps.at[j, c], tap_sem.at[j, c]
            )
            tap_copies.append(copy)
    tap_copies[0].start()
    for copy in tables:
        copy.wait()
    strip = [strips_ref[j, block] for j in range(beams)]
    for j in range(beams):
        safe = jnp.maximum(strip[j], 0)
        for t in range(tiles):
            pltpu.make_async_copy(panel_hbm.at[0, ranges_ref[t, safe]], rows.at[j, t], row_sem.at[j]).start()
        for c in range(2):
            if j + c:
                tap_copies[2 * j + c].start()

    shift = jnp.int32(0)
    for j in range(beams):
        shift = jnp.where(strip[j] >= 0, strip[j] + 1 - j - block, shift)
    base = 2 * shift + 3
    slots[...] = jnp.zeros_like(slots)

    for j in range(beams):
        pltpu.make_async_copy(panel_hbm.at[0, 0:tiles], rows.at[j], row_sem.at[j]).wait()
        for c in range(2):
            tap_copies[2 * j + c].wait()

            @pl.when(strip[j] >= 0)
            def _():
                lhs = rows[j].reshape(tiles * tile_rows, span)
                q0 = jnp.dot(lhs, taps[j, c, 0], preferred_element_type=F32).reshape(tiles, 2, tracks, cols)
                q1 = jnp.dot(lhs, taps[j, c, 1], preferred_element_type=F32).reshape(tiles, 2, tracks, cols)
                parts = (q0[:, 0] - q1[:, 1], q1[:, 0] + q0[:, 1])
                many = tiles * tracks
                for k, part in enumerate(parts):
                    part = part.reshape(many, cols).astype(BF16).astype(F32)
                    for q in range(2):
                        slots[base + 2 * j + 2 * c + q, k * many : (k + 1) * many] += part[:, q * half : (q + 1) * half]

    odd = lax.rem(block, 2)
    first = 4 * (1 - odd)
    upward = 8 * (1 - lax.rem(block // 2, 2))
    for k in range(2):
        swap_ref[k] = slots[first + upward + k].astype(BF16)
        swap_ref[2 + k] = slots[first + 8 - upward + k].astype(BF16)
        near_ref[k] = slots[2 + upward + k]
        next_ref[k] = slots[10 - upward + k]
        mid_ref[k] = slots[first + 4 + k].astype(BF16)
        own_ref[k] = slots[6 + k]
    far_ref[...] = slots[jnp.where(odd == 1, 12, 1)].astype(BF16)


def spread(steer_ref, high_ref, low_ref, tiles):
    _, tracks, heights = steer_ref.shape
    n, m = heights * tiles, tiles * tracks
    pick_row = lax.broadcasted_iota(jnp.int32, (n, heights), 0) // tiles
    pick_row = (pick_row == lax.broadcasted_iota(jnp.int32, (n, heights), 1)).astype(BF16)
    pick_col = lax.broadcasted_iota(jnp.int32, (tracks, m), 1) % tracks
    pick_col = (pick_col == lax.broadcasted_iota(jnp.int32, (tracks, m), 0)).astype(BF16)
    same = lax.broadcasted_iota(jnp.int32, (n, m), 0) % tiles
    same = same == lax.broadcasted_iota(jnp.int32, (n, m), 1) // tracks

    def grow(x):
        wide = lax.dot_general(pick_row, x, (((1,), (1,)), ((), ())), preferred_element_type=F32).astype(BF16)
        wide = jnp.dot(wide, pick_col, preferred_element_type=F32)
        return jnp.where(same, wide, 0.0)

    for piece, ref in ((0, high_ref), (1, low_ref)):
        grown = []
        for part in range(2):
            whole = steer_ref[part]
            high = whole.astype(BF16)
            grown.append(grow(high if piece == 0 else (whole - high.astype(F32)).astype(BF16)))
        ref[:n, :m] = grown[0].astype(BF16)
        ref[:n, m:] = (-grown[1]).astype(BF16)
        ref[n:, :m] = grown[1].astype(BF16)
        ref[n:, m:] = grown[0].astype(BF16)


def focus(own_ref, mid_ref, near_ref, next_ref, far_ref, high_ref, low_ref, out_hbm, x_high, x_low, out, sem, steps):
    half = own_ref.shape[2]
    odd = lax.rem(lax.axis_index("track"), 2)
    for k in range(2):
        total = own_ref[k] + mid_ref[k].astype(F32)
        total += near_ref[k].astype(F32) + next_ref[k].astype(F32)
        total += jnp.where(odd == k, far_ref[...].astype(F32), 0.0)
        high = total.astype(BF16)
        x_high[:, k * half : (k + 1) * half] = high
        x_low[:, k * half : (k + 1) * half] = (total - high.astype(F32)).astype(BF16)

    lines, tiles, width = out.shape
    part = lines // steps
    copies = []
    for i in range(steps):
        at = slice(i * part * tiles, (i + 1) * part * tiles)
        a_high, a_low = high_ref[at], low_ref[at]
        sums = jnp.dot(a_high, x_high[...], preferred_element_type=F32)
        sums += jnp.dot(a_low, x_high[...], preferred_element_type=F32)
        sums += jnp.dot(a_high, x_low[...], preferred_element_type=F32)
        here = pl.ds(i * part, part)
        out[here] = sums.reshape(part, tiles, width)
        copy = pltpu.make_async_copy(out.at[here], out_hbm.at[here], sem.at[i])
        copy.start()
        copies.append(copy)
    for copy in copies:
        copy.wait()


def placed_in(x, name):
    return pltpu.with_memory_space_constraint(x, pltpu.MemorySpace[name])


def body(panels, kernel, steering, beam_strips, range_blocks):
    peers = lax.axis_size("track")
    blocks = beam_strips.shape[0]
    beams, _, span, footprint = kernel.shape
    tiles = range_blocks.shape[1]
    tracks = panels.shape[3]
    heights = steering.shape[1]
    half = footprint // 4
    rows = 2 * tiles * tracks

    def halves(count, dtype):
        return jax.ShapeDtypeStruct((count, rows, half), dtype)

    def send(x, to):
        return lax.ppermute(x, "track", [(i, to(i)) for i in range(peers) if 0 <= to(i) < peers])

    swap, mid, far, near, own, nxt = pl.pallas_call(
        backproject,
        out_shape=(
            halves(4, BF16), halves(2, BF16), jax.ShapeDtypeStruct((rows, half), BF16),
            halves(2, F32), halves(2, F32), halves(2, F32),
        ),
        in_specs=[HBM_SPEC] * 4,
        out_specs=(VMEM_SPEC,) * 6,
        scratch_shapes=[
            pltpu.SMEM((beams, blocks), jnp.int32),
            pltpu.SMEM((tiles, blocks), jnp.int32),
            pltpu.VMEM((beams, tiles, 2, tracks, span), BF16),
            pltpu.VMEM((beams, 2, 2, span, footprint // 2), BF16),
            pltpu.VMEM((14, rows, half), F32),
            pltpu.SemaphoreType.DMA((2,)),
            pltpu.SemaphoreType.DMA((beams,)),
            pltpu.SemaphoreType.DMA((beams, 2)),
        ],
        compiler_params=pltpu.CompilerParams(vmem_limit_bytes=48 << 20),
        cost_estimate=pl.CostEstimate(
            flops=2 * 2 * beams * rows * span * footprint, bytes_accessed=16 << 20, transcendentals=0
        ),
    )(*(placed_in(x, "HBM") for x in (beam_strips.T, range_blocks.T, panels, kernel)))

    swapped = send(swap, lambda i: i ^ 1)
    far_got = send(far, lambda i: i + 3 if i % 2 else i - 3)
    next_sum = (nxt + swapped[2:4].astype(F32)).astype(BF16)
    near_sum = (near + swapped[0:2].astype(F32)).astype(BF16)
    next_got = send(next_sum, lambda i: i + 2 if i // 2 % 2 else i - 2)
    near_got = send(near_sum, lambda i: i - 2 if i // 2 % 2 else i + 2)
    mid_got = send(mid, lambda i: i ^ 1)

    big = jax.ShapeDtypeStruct((2 * heights * tiles, rows), BF16)
    high, low = pl.pallas_call(
        functools.partial(spread, tiles=tiles),
        out_shape=(big, big),
        in_specs=[VMEM_SPEC],
        out_specs=(VMEM_SPEC, VMEM_SPEC),
        compiler_params=pltpu.CompilerParams(vmem_limit_bytes=12 << 20),
        cost_estimate=pl.CostEstimate(flops=200_000_000, bytes_accessed=1 << 20, transcendentals=0),
    )(steering.transpose(0, 2, 1))

    steps = 4
    shape = (2 * heights, tiles, 2 * half)
    volume = pl.pallas_call(
        functools.partial(focus, steps=steps),
        out_shape=jax.ShapeDtypeStruct(shape, F32),
        in_specs=[VMEM_SPEC] * 7,
        out_specs=HBM_SPEC,
        scratch_shapes=[
            pltpu.VMEM((rows, 2 * half), BF16),
            pltpu.VMEM((rows, 2 * half), BF16),
            pltpu.VMEM(shape, F32),
            pltpu.SemaphoreType.DMA((steps,)),
        ],
        compiler_params=pltpu.CompilerParams(vmem_limit_bytes=12 << 20),
        cost_estimate=pl.CostEstimate(flops=400_000_000, bytes_accessed=2 << 20, transcendentals=0),
    )(*(placed_in(x, "VMEM") for x in (own, mid_got, near_got, next_got, far_got, high, low)))
    return volume.reshape(2, heights, tiles, 2 * half)


def solution(mesh):
    placed = (
        P(("scene", "track"), None, None, None, None),
        P(),
        P(),
        P("scene", None),
        P("scene", None),
    )
    return jax.shard_map(
        body, mesh=mesh, in_specs=placed, out_specs=P(None, None, "scene", "track"), check_vma=False
    )
```

profile of v0, /device:TPU:15, one launch (start us, length us, event | category | flops | bytes accessed | tf_op | source)
XLA Modules:
  0.0 22.3 jit_solution(5359834477639937788)
XLA Ops:
  0.0 0.0 copy-start
  0.0 7.5 %shard_map.55 = (bf16[4,256,128]{2,1,0:T(8,128)(2,1)S(1)}, bf16[2,256,128]{2,1,0:T(8,128)(2,1)S(1)}, bf16[256,128]{1,0:T(8,128)(2,1)S(1)}, f32[2,256,128]{2,1,0:...) custom-call(s32[3,16]{1,0:T(4,128)} %bitcast.6, s32[8,16]{1,0:T(8,128)} %bitcast.5, ...), custom_call_target="tpu_custom_call" | custom-call | flops 3221225472 | bytes 16777216 | tf_op jit(solution)/shard_map/pallas_call | solution.py:167
  7.5 1.0 %collective-permute-start.1 = (bf16[4,256,128]{2,1,0:T(8,128)(2,1)S(1)}, bf16[4,256,128]{2,1,0:T(8,128)(2,1)S(1)}, u32[]{:S(2)}, u32[]{:S(2)}) collective-permute-start(bf16[4,256,128]{2,1,0:T(8,128)(2,1)S(1)} %get-tuple-element.16), channel_id=1, source_target_pairs={{0,1},{1,0},{2,3},{3,2},{4,5},{5,4},{6,7},{7,6},{8,9},{9,8},{10,11... | collective-permute-start | bytes 786440 | tf_op jit(solution)/shard_map/ppermute | solution.py:165
  8.5 0.1 collective-permute-start
  8.6 1.1 %collective-permute-done.1 = bf16[4,256,128]{2,1,0:T(8,128)(2,1)S(1)} collective-permute-done((bf16[4,256,128]{2,1,0:T(8,128)(2,1)S(1)}, bf16[4,256,128]{2,1,0:T(8,128)(2,1)S(1)}, u32[]{:S(2)}, u32[]{:S(2)}) %collective-permute-start.1) | collective-permute-done | bytes 262176 | tf_op jit(solution)/shard_map/ppermute | solution.py:165
  9.7 0.1 add_convert_fusion
  9.8 2.8 %collective-permute-start.3 = (bf16[2,256,128]{2,1,0:T(8,128)(2,1)S(1)}, bf16[2,256,128]{2,1,0:T(8,128)(2,1)S(1)}, u32[]{:S(2)}, u32[]{:S(2)}) collective-permute-start(bf16[2,256,128]{2,1,0:T(8,128)(2,1)S(1)} %get-tuple-element.21), channel_id=1, source_target_pairs={{2,4},{3,5},{4,2},{5,3},{6,8},{7,9},{8,6},{9,7},{10,12},{11,13},{1... | collective-permute-start | bytes 393224 | tf_op jit(solution)/shard_map/ppermute | solution.py:165
  12.6 0.1 collective-permute-start.2
  12.8 4.4 %collective-permute-start.4 = (bf16[256,128]{1,0:T(8,128)(2,1)S(1)}, bf16[256,128]{1,0:T(8,128)(2,1)S(1)}, u32[]{:S(2)}, u32[]{:S(2)}) collective-permute-start(bf16[256,128]{1,0:T(8,128)(2,1)S(1)} %get-tuple-element.18), channel_id=1, source_target_pairs={{1,4},{3,6},{4,1},{5,8},{6,3},{7,10},{8,5},{9,12},{10,7},{11,14},{... | collective-permute-start | bytes 196616 | tf_op jit(solution)/shard_map/ppermute | solution.py:165
  17.1 0.0 copy-done
  17.1 0.6 %shard_map.56 = (bf16[1024,256]{1,0:T(8,128)(2,1)S(1)}, bf16[1024,256]{1,0:T(8,128)(2,1)S(1)}) custom-call(f32[2,16,64]{2,1,0:T(8,128)S(1)} %bitcast.4), custom_call_target="tpu_custom_call" | custom-call | flops 200000000 | bytes 1048576 | tf_op jit(solution)/shard_map/pallas_call | solution.py:200
  17.8 1.6 %collective-permute-done.4.far_ref = bf16[256,128]{1,0:T(8,128)(2,1)S(1)} collective-permute-done((bf16[256,128]{1,0:T(8,128)(2,1)S(1)}, bf16[256,128]{1,0:T(8,128)(2,1)S(1)}, u32[]{:S(2)}, u32[]{:S(2)}) %collective-permute-start.4) | collective-permute-done | bytes 65568 | tf_op jit(solution)/shard_map/ppermute | solution.py:165
  19.4 0.0 collective-permute-done.mid_ref
  19.4 0.0 collective-permute-done.3.next_ref
  19.4 1.4 %collective-permute-done.2.near_ref = bf16[2,256,128]{2,1,0:T(8,128)(2,1)S(1)} collective-permute-done((bf16[2,256,128]{2,1,0:T(8,128)(2,1)S(1)}, bf16[2,256,128]{2,1,0:T(8,128)(2,1)S(1)}, u32[]{:S(2)}, u32[]{:S(2)}) %collective-permute-start.2) | collective-permute-done | bytes 131104 | tf_op jit(solution)/shard_map/ppermute | solution.py:165
  20.8 1.5 %shard_map.57 = f32[128,8,256]{2,1,0:T(8,128)} custom-call(f32[2,256,128]{2,1,0:T(8,128)S(1)} %get-tuple-element.13.own_ref, bf16[2,256,128]{2,1,0:T(8,128)(2,1)S(1)} %collective-permute-done.mid_ref, bf16[2,256,128]{2,1,0:T(8,128)(2,1)S(1)} %collective-permute-done.2.near_ref, bf16[2,256,128]{2,1,0:T(8,128)(2,1)S(1)} %collective-permute-done.3.next_ref, ...), custom_call_target="tpu_custom_call" | custom-call | flops 400000000 | bytes 2097152 | tf_op jit(solution)/shard_map/pallas_call | solution.py:211
Async XLA Ops:
  0.0 17.1 %copy-start = (f32[2,64,16]{1,2,0:T(8,128)S(1)}, f32[2,64,16]{1,2,0:T(8,128)}, u32[]{:S(2)}) copy-start(f32[2,64,16]{1,2,0:T(8,128)} %param.7) | copy-start | bytes 24580
  7.5 2.2 %collective-permute-start.1 = (bf16[4,256,128]{2,1,0:T(8,128)(2,1)S(1)}, bf16[4,256,128]{2,1,0:T(8,128)(2,1)S(1)}, u32[]{:S(2)}, u32[]{:S(2)}) collective-permute-start(bf16[4,256,128]{2,1,0:T(8,128)(2,1)S(1)} %get-tuple-element.16), channel_id=1, source_target_pairs={{0,1},{1,0},{2,3},{3,2},{4,5},{5,4},{6,7},{7,6},{8,9},{9,8},{10,11... | collective-permute-start | bytes 786440 | tf_op jit(solution)/shard_map/ppermute | solution.py:165
  8.5 10.8 %collective-permute-start = (bf16[2,256,128]{2,1,0:T(8,128)(2,1)S(1)}, bf16[2,256,128]{2,1,0:T(8,128)(2,1)S(1)}, u32[]{:S(2)}, u32[]{:S(2)}) collective-permute-start(bf16[2,256,128]{2,1,0:T(8,128)(2,1)S(1)} %get-tuple-element.14), channel_id=1, source_target_pairs={{0,1},{1,0},{2,3},{3,2},{4,5},{5,4},{6,7},{7,6},{8,9},{9,8},{10,11... | collective-permute-start | bytes 393224 | tf_op jit(solution)/shard_map/ppermute | solution.py:165
  9.8 9.6 %collective-permute-start.3 = (bf16[2,256,128]{2,1,0:T(8,128)(2,1)S(1)}, bf16[2,256,128]{2,1,0:T(8,128)(2,1)S(1)}, u32[]{:S(2)}, u32[]{:S(2)}) collective-permute-start(bf16[2,256,128]{2,1,0:T(8,128)(2,1)S(1)} %get-tuple-element.21), channel_id=1, source_target_pairs={{2,4},{3,5},{4,2},{5,3},{6,8},{7,9},{8,6},{9,7},{10,12},{11,13},{1... | collective-permute-start | bytes 393224 | tf_op jit(solution)/shard_map/ppermute | solution.py:165
  12.6 8.2 %collective-permute-start.2 = (bf16[2,256,128]{2,1,0:T(8,128)(2,1)S(1)}, bf16[2,256,128]{2,1,0:T(8,128)(2,1)S(1)}, u32[]{:S(2)}, u32[]{:S(2)}) collective-permute-start(bf16[2,256,128]{2,1,0:T(8,128)(2,1)S(1)} %get-tuple-element.22), channel_id=1, source_target_pairs={{0,2},{1,3},{2,0},{3,1},{4,6},{5,7},{6,4},{7,5},{8,10},{9,11},{10,... | collective-permute-start | bytes 393224 | tf_op jit(solution)/shard_map/ppermute | solution.py:165
  12.8 6.6 %collective-permute-start.4 = (bf16[256,128]{1,0:T(8,128)(2,1)S(1)}, bf16[256,128]{1,0:T(8,128)(2,1)S(1)}, u32[]{:S(2)}, u32[]{:S(2)}) collective-permute-start(bf16[256,128]{1,0:T(8,128)(2,1)S(1)} %get-tuple-element.18), channel_id=1, source_target_pairs={{1,4},{3,6},{4,1},{5,8},{6,3},{7,10},{8,5},{9,12},{10,7},{11,14},{... | collective-permute-start | bytes 196616 | tf_op jit(solution)/shard_map/ppermute | solution.py:165
where the time goes:
time: 22.6 us; the launch traced here: 22.3 us
  Pallas kernels  9.66 us (43%)
  starting transfers between devices  8.41 us (37%)
  waiting for transfers between devices  4.1 us (18%)
    ppermute x5, starting transfers between devices, send(): lax.ppermute(x, 'track', [(i, to(i)) for i in range(peers) if 0 <= to(i)...  8.41 us
    pallas_call x1, Pallas kernels, body(): pl.pallas_call(backproject, out_shape=(halves(4, BF16), halves(2, BF16),...  7.54 us
    ppermute x5, waiting for transfers between devices, send(): lax.ppermute(x, 'track', [(i, to(i)) for i in range(peers) if 0 <= to(i)...  4.1 us
    pallas_call x1, Pallas kernels, body(): pl.pallas_call(functools.partial(focus, steps=steps), out_shape=jax.Shape...  1.49 us
    pallas_call x1, Pallas kernels, body(): pl.pallas_call(functools.partial(spread, tiles=tiles), out_shape=(big, bi...  0.63 us
  transfers between devices with their start and end apart: 5, of which 3 were waited for; matrix products, arithmetic and copies ran while one was open for 0% of the time, Pallas kernels for 3%

commit v1 on v0

--- a/solution.py
+++ b/solution.py
@@ -16,8 +16,8 @@
 
 def backproject(
     strips_hbm, ranges_hbm, panel_hbm, kernel_hbm,
-    swap_ref, mid_ref, far_ref, near_ref, own_ref, next_ref,
-    strips_ref, ranges_ref, rows, taps, slots, table_sem, row_sem, tap_sem,
+    swap_ref, mid_ref, far_ref, near_ref, own_ref, next_ref, own_rows, centre,
+    strips_ref, ranges_ref, rows, edges, middles, slots, table_sem, row_sem, tap_sem,
 ):
     block = lax.axis_index("track")
     beams, _, span, footprint = kernel_hbm.shape
@@ -25,7 +25,8 @@
     tracks = panel_hbm.shape[3]
     half = footprint // 4
     cols = footprint // 2
-    tile_rows = 2 * tracks
+    many = tiles * tracks
+    inner = slice(half, half + cols)
 
     tables = [
         pltpu.make_async_copy(strips_hbm, strips_ref, table_sem.at[0]),
@@ -33,47 +34,72 @@
     ]
     for copy in tables:
         copy.start()
-    tap_copies = []
-    for j in range(beams):
-        for c in range(2):
-            copy = pltpu.make_async_copy(
-                kernel_hbm.at[j, :, :, c * cols : (c + 1) * cols], taps.at[j, c], tap_sem.at[j, c]
-            )
-            tap_copies.append(copy)
-    tap_copies[0].start()
+
+    def fetch_edges(j):
+        for k, q in enumerate((0, 3)):
+            pltpu.make_async_copy(
+                kernel_hbm.at[j, :, :, q * half : (q + 1) * half],
+                edges.at[j, :, :, k * half : (k + 1) * half],
+                tap_sem.at[j],
+            ).start()
+
+    order = [beams // 2] + [j for j in range(beams) if j != beams // 2]
+    fetch_edges(order[0])
     for copy in tables:
         copy.wait()
     strip = [strips_ref[j, block] for j in range(beams)]
-    for j in range(beams):
-        safe = jnp.maximum(strip[j], 0)
-        for t in range(tiles):
-            pltpu.make_async_copy(panel_hbm.at[0, ranges_ref[t, safe]], rows.at[j, t], row_sem.at[j]).start()
-        for c in range(2):
-            if j + c:
-                tap_copies[2 * j + c].start()
-
     shift = jnp.int32(0)
     for j in range(beams):
         shift = jnp.where(strip[j] >= 0, strip[j] + 1 - j - block, shift)
     base = 2 * shift + 3
+    mine = 1 - shift
+    for j in order:
+        safe = jnp.maximum(strip[j], 0)
+        for t in range(tiles):
+            pltpu.make_async_copy(panel_hbm.at[0, ranges_ref[t, safe]], rows.at[j, t], row_sem.at[j]).start()
+        if j != order[0]:
+            fetch_edges(j)
+    for j in order:
+
+        @pl.when(j != mine)
+        def _():
+            pltpu.make_async_copy(kernel_hbm.at[j, :, :, inner], middles.at[j], tap_sem.at[beams + j]).start()
+
+    for t in range(tiles):
+        pltpu.make_async_copy(panel_hbm.at[0, ranges_ref[t, block]], own_rows.at[t], row_sem.at[beams]).start()
+    last = pltpu.make_async_copy(kernel_hbm.at[mine, :, :, inner], centre, tap_sem.at[2 * beams])
+    last.start()
     slots[...] = jnp.zeros_like(slots)
 
-    for j in range(beams):
+    def add(lhs, taps, targets):
+        q0 = jnp.dot(lhs, taps[0], preferred_element_type=F32).reshape(tiles, 2, tracks, cols)
+        q1 = jnp.dot(lhs, taps[1], preferred_element_type=F32).reshape(tiles, 2, tracks, cols)
+        parts = (q0[:, 0] - q1[:, 1], q1[:, 0] + q0[:, 1])
+        for k, part in enumerate(parts):
+            part = part.reshape(many, cols).astype(BF16).astype(F32)
+            for n, target in enumerate(targets):
+                slots[target, k * many : (k + 1) * many] += part[:, n * half : (n + 1) * half]
+
+    for j in order:
         pltpu.make_async_copy(panel_hbm.at[0, 0:tiles], rows.at[j], row_sem.at[j]).wait()
-        for c in range(2):
-            tap_copies[2 * j + c].wait()
-
-            @pl.when(strip[j] >= 0)
-            def _():
-                lhs = rows[j].reshape(tiles * tile_rows, span)
-                q0 = jnp.dot(lhs, taps[j, c, 0], preferred_element_type=F32).reshape(tiles, 2, tracks, cols)
-                q1 = jnp.dot(lhs, taps[j, c, 1], preferred_element_type=F32).reshape(tiles, 2, tracks, cols)
-                parts = (q0[:, 0] - q1[:, 1], q1[:, 0] + q0[:, 1])
-                many = tiles * tracks
-                for k, part in enumerate(parts):
-                    part = part.reshape(many, cols).astype(BF16).astype(F32)
-                    for q in range(2):
-                        slots[base + 2 * j + 2 * c + q, k * many : (k + 1) * many] += part[:, q * half : (q + 1) * half]
+        pltpu.make_async_copy(kernel_hbm.at[j, :, :, inner], edges.at[j], tap_sem.at[j]).wait()
+
+        @pl.when(strip[j] >= 0)
+        def _():
+            lhs = rows[j].reshape(2 * many, span)
+            add(lhs, edges.at[j], (base + 2 * j, base + 2 * j + 3))
+
+    for j in order:
+        whole = pltpu.make_async_copy(kernel_hbm.at[j, :, :, inner], middles.at[j], tap_sem.at[beams + j])
+
+        @pl.when(j != mine)
+        def _():
+            whole.wait()
+
+        @pl.when((j != mine) & (strip[j] >= 0))
+        def _():
+            lhs = rows[j].reshape(2 * many, span)
+            add(lhs, middles.at[j], (base + 2 * j + 1, base + 2 * j + 2))
 
     odd = lax.rem(block, 2)
     first = 4 * (1 - odd)
@@ -86,6 +112,24 @@
         mid_ref[k] = slots[first + 4 + k].astype(BF16)
         own_ref[k] = slots[6 + k]
     far_ref[...] = slots[jnp.where(odd == 1, 12, 1)].astype(BF16)
+    pltpu.make_async_copy(panel_hbm.at[0, 0:tiles], own_rows, row_sem.at[beams]).wait()
+    last.wait()
+
+
+def finish_own(rows, centre, own_ref, out_ref):
+    tiles, _, tracks, span = rows.shape
+    cols = centre.shape[2]
+    half = cols // 2
+    many = tiles * tracks
+    lhs = rows[...].reshape(2 * many, span)
+    q0 = jnp.dot(lhs, centre[0], preferred_element_type=F32).reshape(tiles, 2, tracks, cols)
+    q1 = jnp.dot(lhs, centre[1], preferred_element_type=F32).reshape(tiles, 2, tracks, cols)
+    parts = (q0[:, 0] - q1[:, 1], q1[:, 0] + q0[:, 1])
+    for k, part in enumerate(parts):
+        part = part.reshape(many, cols).astype(BF16).astype(F32)
+        at = slice(k * many, (k + 1) * many)
+        for n in range(2):
+            out_ref[n, at] = own_ref[n, at] + part[:, n * half : (n + 1) * half]
 
 
 def spread(steer_ref, high_ref, low_ref, tiles):
@@ -164,25 +208,28 @@
     def send(x, to):
         return lax.ppermute(x, "track", [(i, to(i)) for i in range(peers) if 0 <= to(i) < peers])
 
-    swap, mid, far, near, own, nxt = pl.pallas_call(
+    swap, mid, far, near, own, nxt, picked, centre = pl.pallas_call(
         backproject,
         out_shape=(
             halves(4, BF16), halves(2, BF16), jax.ShapeDtypeStruct((rows, half), BF16),
             halves(2, F32), halves(2, F32), halves(2, F32),
+            jax.ShapeDtypeStruct((tiles, 2, tracks, span), BF16),
+            jax.ShapeDtypeStruct((2, span, footprint // 2), BF16),
         ),
         in_specs=[HBM_SPEC] * 4,
-        out_specs=(VMEM_SPEC,) * 6,
+        out_specs=(VMEM_SPEC,) * 8,
         scratch_shapes=[
             pltpu.SMEM((beams, blocks), jnp.int32),
             pltpu.SMEM((tiles, blocks), jnp.int32),
             pltpu.VMEM((beams, tiles, 2, tracks, span), BF16),
-            pltpu.VMEM((beams, 2, 2, span, footprint // 2), BF16),
+            pltpu.VMEM((beams, 2, span, footprint // 2), BF16),
+            pltpu.VMEM((beams, 2, span, footprint // 2), BF16),
             pltpu.VMEM((14, rows, half), F32),
             pltpu.SemaphoreType.DMA((2,)),
-            pltpu.SemaphoreType.DMA((beams,)),
-            pltpu.SemaphoreType.DMA((beams, 2)),
+            pltpu.SemaphoreType.DMA((beams + 1,)),
+            pltpu.SemaphoreType.DMA((2 * beams + 1,)),
         ],
-        compiler_params=pltpu.CompilerParams(vmem_limit_bytes=48 << 20),
+        compiler_params=pltpu.CompilerParams(vmem_limit_bytes=24 << 20),
         cost_estimate=pl.CostEstimate(
             flops=2 * 2 * beams * rows * span * footprint, bytes_accessed=16 << 20, transcendentals=0
         ),
@@ -205,6 +252,15 @@
         compiler_params=pltpu.CompilerParams(vmem_limit_bytes=12 << 20),
         cost_estimate=pl.CostEstimate(flops=200_000_000, bytes_accessed=1 << 20, transcendentals=0),
     )(steering.transpose(0, 2, 1))
+
+    own = pl.pallas_call(
+        finish_own,
+        out_shape=halves(2, F32),
+        in_specs=[VMEM_SPEC] * 3,
+        out_specs=VMEM_SPEC,
+        compiler_params=pltpu.CompilerParams(vmem_limit_bytes=12 << 20),
+        cost_estimate=pl.CostEstimate(flops=2 * rows * span * footprint, bytes_accessed=1 << 20, transcendentals=0),
+    )(*(placed_in(x, "VMEM") for x in (picked, centre, own)))
 
     steps = 4
     shape = (2 * heights, tiles, 2 * half)

time: 22.6 us -> 20.8 us (0.920)
  waiting for transfers between devices: 4.1 us -> 1.95 us
  starting transfers between devices: 8.41 us -> 9.11 us
    ppermute x5, waiting for transfers between devices: 4.1 us -> 1.95 us  [send(): lax.ppermute(x, 'track', [(i, to(i)) for i in range(peers) if 0 <= to(i)...]
    pallas_call x1, Pallas kernels: 7.54 us -> 6.62 us  [body(): pl.pallas_call(backproject, out_shape=(halves(4, BF16), halves(2, BF16),...]
    pallas_call x0 -> x1, Pallas kernels: none -> 0.71 us  [body(): pl.pallas_call(finish_own, out_shape=halves(2, F32), in_specs=[VMEM_SPEC]...]
    ppermute x5, starting transfers between devices: 8.41 us -> 9.11 us  [send(): lax.ppermute(x, 'track', [(i, to(i)) for i in range(peers) if 0 <= to(i)...]
  transfers between devices with their start and end apart: 5 -> 5, of which waited for: 3 -> 2; matrix products, arithmetic and copies ran while one was open for 0% -> 0% of each run, Pallas kernels for 3% -> 6%
where the time goes in v1:
time: 20.8 us; the launch traced here: 20.7 us
  Pallas kernels  9.47 us (46%)
  starting transfers between devices  9.11 us (44%)
  waiting for transfers between devices  1.95 us (9%)
    ppermute x5, starting transfers between devices, send(): lax.ppermute(x, 'track', [(i, to(i)) for i in range(peers) if 0 <= to(i)...  9.11 us
    pallas_call x1, Pallas kernels, body(): pl.pallas_call(backproject, out_shape=(halves(4, BF16), halves(2, BF16),...  6.62 us
    ppermute x5, waiting for transfers between devices, send(): lax.ppermute(x, 'track', [(i, to(i)) for i in range(peers) if 0 <= to(i)...  1.95 us
    pallas_call x1, Pallas kernels, body(): pl.pallas_call(functools.partial(focus, steps=steps), out_shape=jax.Shape...  1.5 us
    pallas_call x1, Pallas kernels, body(): pl.pallas_call(finish_own, out_shape=halves(2, F32), in_specs=[VMEM_SPEC]...  0.71 us
    pallas_call x1, Pallas kernels, body(): pl.pallas_call(functools.partial(spread, tiles=tiles), out_shape=(big, bi...  0.63 us
  transfers between devices with their start and end apart: 5, of which 2 were waited for; matrix products, arithmetic and copies ran while one was open for 0% of the time, Pallas kernels for 6%

profile of v1, /device:TPU:15, one launch (start us, length us, event | category | flops | bytes accessed | tf_op | source)
XLA Modules:
  0.0 20.7 jit_solution(16570295698622319089)
XLA Ops:
  0.0 0.0 copy-start
  0.0 6.6 %shard_map.55 = (bf16[4,256,128]{2,1,0:T(8,128)(2,1)S(1)}, bf16[2,256,128]{2,1,0:T(8,128)(2,1)S(1)}, bf16[256,128]{1,0:T(8,128)(2,1)S(1)}, f32[2,256,128]{2,1,0:...) custom-call(s32[3,16]{1,0:T(4,128)} %bitcast.6, ...), custom_call_target="tpu_custom_call" | custom-call | flops 3221225472 | bytes 16777216 | tf_op jit(solution)/shard_map/pallas_call | solution.py:211
  6.6 0.8 %collective-permute-start.1 = (bf16[4,256,128]{2,1,0:T(8,128)(2,1)S(1)}, bf16[4,256,128]{2,1,0:T(8,128)(2,1)S(1)}, u32[]{:S(2)}, u32[]{:S(2)}) collective-permute-start(bf16[4,256,128]{2,1,0:T(8,128)(2,1)S(1)} %get-tuple-element.20), channel_id=1, source_target_pairs={{0,1},{1,0},{2,3},{3,2},{4,5},{5,4},{6,7},{7,6},{8,9},{9,8},{10,11... | collective-permute-start | bytes 786440 | tf_op jit(solution)/shard_map/ppermute | solution.py:209
  7.4 0.1 collective-permute-start
  7.5 1.1 %collective-permute-done.1 = bf16[4,256,128]{2,1,0:T(8,128)(2,1)S(1)} collective-permute-done((bf16[4,256,128]{2,1,0:T(8,128)(2,1)S(1)}, bf16[4,256,128]{2,1,0:T(8,128)(2,1)S(1)}, u32[]{:S(2)}, u32[]{:S(2)}) %collective-permute-start.1) | collective-permute-done | bytes 262176 | tf_op jit(solution)/shard_map/ppermute | solution.py:209
  8.6 0.1 add_convert_fusion
  8.7 0.2 %collective-permute-start.2 = (bf16[2,256,128]{2,1,0:T(8,128)(2,1)S(1)}, bf16[2,256,128]{2,1,0:T(8,128)(2,1)S(1)}, u32[]{:S(2)}, u32[]{:S(2)}) collective-permute-start(bf16[2,256,128]{2,1,0:T(8,128)(2,1)S(1)} %get-tuple-element.26), channel_id=1, source_target_pairs={{0,2},{1,3},{2,0},{3,1},{4,6},{5,7},{6,4},{7,5},{8,10},{9,11},{10,... | collective-permute-start | bytes 393224 | tf_op jit(solution)/shard_map/ppermute | solution.py:209
  8.9 4.1 %collective-permute-start.3 = (bf16[2,256,128]{2,1,0:T(8,128)(2,1)S(1)}, bf16[2,256,128]{2,1,0:T(8,128)(2,1)S(1)}, u32[]{:S(2)}, u32[]{:S(2)}) collective-permute-start(bf16[2,256,128]{2,1,0:T(8,128)(2,1)S(1)} %get-tuple-element.25), channel_id=1, source_target_pairs={{2,4},{3,5},{4,2},{5,3},{6,8},{7,9},{8,6},{9,7},{10,12},{11,13},{1... | collective-permute-start | bytes 393224 | tf_op jit(solution)/shard_map/ppermute | solution.py:209
  13.1 3.8 %collective-permute-start.4 = (bf16[256,128]{1,0:T(8,128)(2,1)S(1)}, bf16[256,128]{1,0:T(8,128)(2,1)S(1)}, u32[]{:S(2)}, u32[]{:S(2)}) collective-permute-start(bf16[256,128]{1,0:T(8,128)(2,1)S(1)} %get-tuple-element.22), channel_id=1, source_target_pairs={{1,4},{3,6},{4,1},{5,8},{6,3},{7,10},{8,5},{9,12},{10,7},{11,14},{... | collective-permute-start | bytes 196616 | tf_op jit(solution)/shard_map/ppermute | solution.py:209
  16.9 0.0 copy-done
  16.9 0.6 %shard_map.57 = (bf16[1024,256]{1,0:T(8,128)(2,1)S(1)}, bf16[1024,256]{1,0:T(8,128)(2,1)S(1)}) custom-call(f32[2,16,64]{2,1,0:T(8,128)S(1)} %bitcast.4), custom_call_target="tpu_custom_call" | custom-call | flops 200000000 | bytes 1048576 | tf_op jit(solution)/shard_map/pallas_call | solution.py:247
  17.6 0.7 %shard_map.56.own_ref = f32[2,256,128]{2,1,0:T(8,128)S(1)} custom-call(bf16[8,2,16,2048]{3,2,1,0:T(8,128)(2,1)S(1)} %get-tuple-element.15.rows, bf16[2,2048,256]{2,1,0:T(8,128)(2,1)S(1)} %get-tuple-element.16.centre, f32[2,256,128]{2,1,0:T(8,128)S(1)} %get-tuple-element.17.own_ref), custom_call_target="tpu_custom_call" | custom-call | flops 536870912 | bytes 1048576 | tf_op jit(solution)/shard_map/pallas_call | solution.py:256
  18.3 0.9 %collective-permute-done.4.far_ref = bf16[256,128]{1,0:T(8,128)(2,1)S(1)} collective-permute-done((bf16[256,128]{1,0:T(8,128)(2,1)S(1)}, bf16[256,128]{1,0:T(8,128)(2,1)S(1)}, u32[]{:S(2)}, u32[]{:S(2)}) %collective-permute-start.4) | collective-permute-done | bytes 65568 | tf_op jit(solution)/shard_map/ppermute | solution.py:209
  19.1 0.0 collective-permute-done.mid_ref
  19.1 0.0 collective-permute-done.2.near_ref
  19.1 0.0 collective-permute-done.3.next_ref
  19.2 1.5 %shard_map.58 = f32[128,8,256]{2,1,0:T(8,128)} custom-call(f32[2,256,128]{2,1,0:T(8,128)S(1)} %shard_map.56.own_ref, bf16[2,256,128]{2,1,0:T(8,128)(2,1)S(1)} %collective-permute-done.mid_ref, bf16[2,256,128]{2,1,0:T(8,128)(2,1)S(1)} %collective-permute-done.2.near_ref, bf16[2,256,128]{2,1,0:T(8,128)(2,1)S(1)} %collective-permute-done.3.next_ref, ...), custom_call_target="tpu_custom_call" | custom-call | flops 400000000 | bytes 2097152 | tf_op jit(solution)/shard_map/pallas_call | solution.py:267
Async XLA Ops:
  0.0 16.9 %copy-start = (f32[2,64,16]{1,2,0:T(8,128)S(1)}, f32[2,64,16]{1,2,0:T(8,128)}, u32[]{:S(2)}) copy-start(f32[2,64,16]{1,2,0:T(8,128)} %param.7) | copy-start | bytes 24580
  6.6 1.9 %collective-permute-start.1 = (bf16[4,256,128]{2,1,0:T(8,128)(2,1)S(1)}, bf16[4,256,128]{2,1,0:T(8,128)(2,1)S(1)}, u32[]{:S(2)}, u32[]{:S(2)}) collective-permute-start(bf16[4,256,128]{2,1,0:T(8,128)(2,1)S(1)} %get-tuple-element.20), channel_id=1, source_target_pairs={{0,1},{1,0},{2,3},{3,2},{4,5},{5,4},{6,7},{7,6},{8,9},{9,8},{10,11... | collective-permute-start | bytes 786440 | tf_op jit(solution)/shard_map/ppermute | solution.py:209
  7.4 11.7 %collective-permute-start = (bf16[2,256,128]{2,1,0:T(8,128)(2,1)S(1)}, bf16[2,256,128]{2,1,0:T(8,128)(2,1)S(1)}, u32[]{:S(2)}, u32[]{:S(2)}) collective-permute-start(bf16[2,256,128]{2,1,0:T(8,128)(2,1)S(1)} %get-tuple-element.18), channel_id=1, source_target_pairs={{0,1},{1,0},{2,3},{3,2},{4,5},{5,4},{6,7},{7,6},{8,9},{9,8},{10,11... | collective-permute-start | bytes 393224 | tf_op jit(solution)/shard_map/ppermute | solution.py:209
  8.7 10.5 %collective-permute-start.2 = (bf16[2,256,128]{2,1,0:T(8,128)(2,1)S(1)}, bf16[2,256,128]{2,1,0:T(8,128)(2,1)S(1)}, u32[]{:S(2)}, u32[]{:S(2)}) collective-permute-start(bf16[2,256,128]{2,1,0:T(8,128)(2,1)S(1)} %get-tuple-element.26), channel_id=1, source_target_pairs={{0,2},{1,3},{2,0},{3,1},{4,6},{5,7},{6,4},{7,5},{8,10},{9,11},{10,... | collective-permute-start | bytes 393224 | tf_op jit(solution)/shard_map/ppermute | solution.py:209
  8.9 10.2 %collective-permute-start.3 = (bf16[2,256,128]{2,1,0:T(8,128)(2,1)S(1)}, bf16[2,256,128]{2,1,0:T(8,128)(2,1)S(1)}, u32[]{:S(2)}, u32[]{:S(2)}) collective-permute-start(bf16[2,256,128]{2,1,0:T(8,128)(2,1)S(1)} %get-tuple-element.25), channel_id=1, source_target_pairs={{2,4},{3,5},{4,2},{5,3},{6,8},{7,9},{8,6},{9,7},{10,12},{11,13},{1... | collective-permute-start | bytes 393224 | tf_op jit(solution)/shard_map/ppermute | solution.py:209
  13.1 6.1 %collective-permute-start.4 = (bf16[256,128]{1,0:T(8,128)(2,1)S(1)}, bf16[256,128]{1,0:T(8,128)(2,1)S(1)}, u32[]{:S(2)}, u32[]{:S(2)}) collective-permute-start(bf16[256,128]{1,0:T(8,128)(2,1)S(1)} %get-tuple-element.22), channel_id=1, source_target_pairs={{1,4},{3,6},{4,1},{5,8},{6,3},{7,10},{8,5},{9,12},{10,7},{11,14},{... | collective-permute-start | bytes 196616 | tf_op jit(solution)/shard_map/ppermute | solution.py:209

commit v2 on v1

--- a/solution.py
+++ b/solution.py
@@ -16,7 +16,7 @@
 
 def backproject(
     strips_hbm, ranges_hbm, panel_hbm, kernel_hbm,
-    swap_ref, mid_ref, far_ref, near_ref, own_ref, next_ref, own_rows, centre,
+    swap_ref, cross_ref, mid_ref, far_ref, near_ref, own_ref, next_ref, own_rows, centre,
     strips_ref, ranges_ref, rows, edges, middles, slots, table_sem, row_sem, tap_sem,
 ):
     block = lax.axis_index("track")
@@ -106,7 +106,7 @@
     upward = 8 * (1 - lax.rem(block // 2, 2))
     for k in range(2):
         swap_ref[k] = slots[first + upward + k].astype(BF16)
-        swap_ref[2 + k] = slots[first + 8 - upward + k].astype(BF16)
+        cross_ref[k] = slots[first + 8 - upward + k].astype(BF16)
         near_ref[k] = slots[2 + upward + k]
         next_ref[k] = slots[10 - upward + k]
         mid_ref[k] = slots[first + 4 + k].astype(BF16)
@@ -132,58 +132,68 @@
             out_ref[n, at] = own_ref[n, at] + part[:, n * half : (n + 1) * half]
 
 
-def spread(steer_ref, high_ref, low_ref, tiles):
+def fold(steer_ref, out_ref):
     _, tracks, heights = steer_ref.shape
-    n, m = heights * tiles, tiles * tracks
-    pick_row = lax.broadcasted_iota(jnp.int32, (n, heights), 0) // tiles
-    pick_row = (pick_row == lax.broadcasted_iota(jnp.int32, (n, heights), 1)).astype(BF16)
-    pick_col = lax.broadcasted_iota(jnp.int32, (tracks, m), 1) % tracks
-    pick_col = (pick_col == lax.broadcasted_iota(jnp.int32, (tracks, m), 0)).astype(BF16)
-    same = lax.broadcasted_iota(jnp.int32, (n, m), 0) % tiles
-    same = same == lax.broadcasted_iota(jnp.int32, (n, m), 1) // tracks
-
-    def grow(x):
-        wide = lax.dot_general(pick_row, x, (((1,), (1,)), ((), ())), preferred_element_type=F32).astype(BF16)
-        wide = jnp.dot(wide, pick_col, preferred_element_type=F32)
-        return jnp.where(same, wide, 0.0)
-
-    for piece, ref in ((0, high_ref), (1, low_ref)):
-        grown = []
-        for part in range(2):
-            whole = steer_ref[part]
-            high = whole.astype(BF16)
-            grown.append(grow(high if piece == 0 else (whole - high.astype(F32)).astype(BF16)))
-        ref[:n, :m] = grown[0].astype(BF16)
-        ref[:n, m:] = (-grown[1]).astype(BF16)
-        ref[n:, :m] = grown[1].astype(BF16)
-        ref[n:, m:] = grown[0].astype(BF16)
-
-
-def focus(own_ref, mid_ref, near_ref, next_ref, far_ref, high_ref, low_ref, out_hbm, x_high, x_low, out, sem, steps):
-    half = own_ref.shape[2]
+    same = lax.broadcasted_iota(jnp.int32, (heights, heights), 0)
+    same = (same == lax.broadcasted_iota(jnp.int32, (heights, heights), 1)).astype(BF16)
+    width = out_ref.shape[1]
+
+    def turned(x):
+        return lax.dot_general(same, x, (((1,), (1,)), ((), ())), preferred_element_type=F32).astype(BF16)
+
+    def put(x, *starts):
+        row = lax.broadcasted_iota(jnp.int32, (tracks, width), 0)
+        col = lax.broadcasted_iota(jnp.int32, (tracks, width), 1)
+        where = functools.reduce(jnp.logical_or, [col == row + start * tracks for start in starts])
+        return jnp.dot(x, where.astype(BF16), preferred_element_type=F32)
+
+    high, low = [], []
+    for part in range(2):
+        whole = steer_ref[part]
+        top = whole.astype(BF16)
+        high.append(turned(top))
+        low.append(turned((whole - top.astype(F32)).astype(BF16)))
+    real = put(high[0], 0, 2) + put(-high[1], 1, 3) + put(low[0], 4) + put(-low[1], 5)
+    imag = put(high[1], 0, 2) + put(high[0], 1, 3) + put(low[1], 4) + put(low[0], 5)
+    out_ref[:heights] = real.astype(BF16)
+    out_ref[heights:] = imag.astype(BF16)
+
+
+def focus(own_ref, mid_ref, near_ref, next_ref, far_ref, matrix_ref, out_hbm, pieces, out, sem):
+    _, lines, tiles, half = out.shape
+    tracks = own_ref.shape[1] // (2 * tiles)
     odd = lax.rem(lax.axis_index("track"), 2)
     for k in range(2):
         total = own_ref[k] + mid_ref[k].astype(F32)
         total += near_ref[k].astype(F32) + next_ref[k].astype(F32)
         total += jnp.where(odd == k, far_ref[...].astype(F32), 0.0)
         high = total.astype(BF16)
-        x_high[:, k * half : (k + 1) * half] = high
-        x_low[:, k * half : (k + 1) * half] = (total - high.astype(F32)).astype(BF16)
-
-    lines, tiles, width = out.shape
-    part = lines // steps
+        low = (total - high.astype(F32)).astype(BF16)
+        cols = slice(k * half, (k + 1) * half)
+        for part in range(2):
+            for tile in range(tiles):
+                start = (part * tiles + tile) * tracks
+                for place, piece in enumerate((high, low, high)):
+                    to = (2 * place + part) * tracks
+                    pieces[tile, to : to + tracks, cols] = piece[start : start + tracks]
+
+    steps = sem.shape[0]
+    count = lines // steps
     copies = []
     for i in range(steps):
-        at = slice(i * part * tiles, (i + 1) * part * tiles)
-        a_high, a_low = high_ref[at], low_ref[at]
-        sums = jnp.dot(a_high, x_high[...], preferred_element_type=F32)
-        sums += jnp.dot(a_low, x_high[...], preferred_element_type=F32)
-        sums += jnp.dot(a_high, x_low[...], preferred_element_type=F32)
-        here = pl.ds(i * part, part)
-        out[here] = sums.reshape(part, tiles, width)
-        copy = pltpu.make_async_copy(out.at[here], out_hbm.at[here], sem.at[i])
-        copy.start()
-        copies.append(copy)
+        matrix = matrix_ref[i * count : (i + 1) * count]
+        for tile in range(tiles):
+            sums = jnp.dot(matrix, pieces[tile], preferred_element_type=F32)
+            for k in range(2):
+                flat = out.at[k].reshape(lines * tiles, half)
+                flat[pl.ds(i * count * tiles + tile, count, stride=tiles)] = sums[:, k * half : (k + 1) * half]
+        here = pl.ds(i * count, count)
+        for k in range(2):
+            copy = pltpu.make_async_copy(
+                out.at[k, here], out_hbm.at[here, :, k * half : (k + 1) * half], sem.at[i, k]
+            )
+            copy.start()
+            copies.append(copy)
     for copy in copies:
         copy.wait()
 
@@ -208,16 +218,16 @@
     def send(x, to):
         return lax.ppermute(x, "track", [(i, to(i)) for i in range(peers) if 0 <= to(i) < peers])
 
-    swap, mid, far, near, own, nxt, picked, centre = pl.pallas_call(
+    swap, cross, mid, far, near, own, nxt, picked, centre = pl.pallas_call(
         backproject,
         out_shape=(
-            halves(4, BF16), halves(2, BF16), jax.ShapeDtypeStruct((rows, half), BF16),
+            halves(2, BF16), halves(2, BF16), halves(2, BF16), jax.ShapeDtypeStruct((rows, half), BF16),
             halves(2, F32), halves(2, F32), halves(2, F32),
             jax.ShapeDtypeStruct((tiles, 2, tracks, span), BF16),
             jax.ShapeDtypeStruct((2, span, footprint // 2), BF16),
         ),
         in_specs=[HBM_SPEC] * 4,
-        out_specs=(VMEM_SPEC,) * 8,
+        out_specs=(VMEM_SPEC,) * 9,
         scratch_shapes=[
             pltpu.SMEM((beams, blocks), jnp.int32),
             pltpu.SMEM((tiles, blocks), jnp.int32),
@@ -236,21 +246,21 @@
     )(*(placed_in(x, "HBM") for x in (beam_strips.T, range_blocks.T, panels, kernel)))
 
     swapped = send(swap, lambda i: i ^ 1)
+    crossed = send(cross, lambda i: i ^ 1)
     far_got = send(far, lambda i: i + 3 if i % 2 else i - 3)
-    next_sum = (nxt + swapped[2:4].astype(F32)).astype(BF16)
-    near_sum = (near + swapped[0:2].astype(F32)).astype(BF16)
+    next_sum = (nxt + crossed.astype(F32)).astype(BF16)
+    near_sum = (near + swapped.astype(F32)).astype(BF16)
     next_got = send(next_sum, lambda i: i + 2 if i // 2 % 2 else i - 2)
     near_got = send(near_sum, lambda i: i - 2 if i // 2 % 2 else i + 2)
     mid_got = send(mid, lambda i: i ^ 1)
 
-    big = jax.ShapeDtypeStruct((2 * heights * tiles, rows), BF16)
-    high, low = pl.pallas_call(
-        functools.partial(spread, tiles=tiles),
-        out_shape=(big, big),
+    matrix = pl.pallas_call(
+        fold,
+        out_shape=jax.ShapeDtypeStruct((2 * heights, 6 * tracks), BF16),
         in_specs=[VMEM_SPEC],
-        out_specs=(VMEM_SPEC, VMEM_SPEC),
+        out_specs=VMEM_SPEC,
         compiler_params=pltpu.CompilerParams(vmem_limit_bytes=12 << 20),
-        cost_estimate=pl.CostEstimate(flops=200_000_000, bytes_accessed=1 << 20, transcendentals=0),
+        cost_estimate=pl.CostEstimate(flops=10_000_000, bytes_accessed=1 << 15, transcendentals=0),
     )(steering.transpose(0, 2, 1))
 
     own = pl.pallas_call(
@@ -262,22 +272,20 @@
         cost_estimate=pl.CostEstimate(flops=2 * rows * span * footprint, bytes_accessed=1 << 20, transcendentals=0),
     )(*(placed_in(x, "VMEM") for x in (picked, centre, own)))
 
-    steps = 4
-    shape = (2 * heights, tiles, 2 * half)
+    steps = 2
     volume = pl.pallas_call(
-        functools.partial(focus, steps=steps),
-        out_shape=jax.ShapeDtypeStruct(shape, F32),
-        in_specs=[VMEM_SPEC] * 7,
+        focus,
+        out_shape=jax.ShapeDtypeStruct((2 * heights, tiles, 2 * half), F32),
+        in_specs=[VMEM_SPEC] * 6,
         out_specs=HBM_SPEC,
         scratch_shapes=[
-            pltpu.VMEM((rows, 2 * half), BF16),
-            pltpu.VMEM((rows, 2 * half), BF16),
-            pltpu.VMEM(shape, F32),
-            pltpu.SemaphoreType.DMA((steps,)),
+            pltpu.VMEM((tiles, 6 * tracks, 2 * half), BF16),
+            pltpu.VMEM((2, 2 * heights, tiles, half), F32),
+            pltpu.SemaphoreType.DMA((steps, 2)),
         ],
         compiler_params=pltpu.CompilerParams(vmem_limit_bytes=12 << 20),
-        cost_estimate=pl.CostEstimate(flops=400_000_000, bytes_accessed=2 << 20, transcendentals=0),
-    )(*(placed_in(x, "VMEM") for x in (own, mid_got, near_got, next_got, far_got, high, low)))
+        cost_estimate=pl.CostEstimate(flops=100_000_000, bytes_accessed=2 << 20, transcendentals=0),
+    )(*(placed_in(x, "VMEM") for x in (own, mid_got, near_got, next_got, far_got, matrix)))
     return volume.reshape(2, heights, tiles, 2 * half)
 
 

time: 20.8 us -> 21.2 us (1.019)
  the two profiles are of different devices: /device:TPU:15 before, /device:TPU:0 now
where the time goes in v2:
time: 21.2 us; the launch traced here: 21.1 us
  Pallas kernels  8.9 us (42%)
  starting transfers between devices  8.13 us (38%)
  waiting for transfers between devices  3.89 us (18%)
    ppermute x6, starting transfers between devices, send(): lax.ppermute(x, 'track', [(i, to(i)) for i in range(peers) if 0 <= to(i)...  8.13 us
    pallas_call x1, Pallas kernels, body(): pl.pallas_call(backproject, out_shape=(halves(2, BF16), halves(2, BF16),...  6.58 us
    ppermute x6, waiting for transfers between devices, send(): lax.ppermute(x, 'track', [(i, to(i)) for i in range(peers) if 0 <= to(i)...  3.89 us
    pallas_call x1, Pallas kernels, body(): pl.pallas_call(focus, out_shape=jax.ShapeDtypeStruct((2 * heights, tiles,...  1.32 us
    pallas_call x1, Pallas kernels, body(): pl.pallas_call(finish_own, out_shape=halves(2, F32), in_specs=[VMEM_SPEC]...  0.71 us
  transfers between devices with their start and end apart: 6, of which 2 were waited for; matrix products, arithmetic and copies ran while one was open for 0% of the time, Pallas kernels for 5%

profile of v2, /device:TPU:0, one launch (start us, length us, event | category | flops | bytes accessed | tf_op | source)
XLA Modules:
  0.0 21.1 jit_solution(5611995597857863026)
XLA Ops:
  0.0 0.0 copy-start
  0.0 6.6 %shard_map.55 = (bf16[2,256,128]{2,1,0:T(8,128)(2,1)S(1)}, bf16[2,256,128]{2,1,0:T(8,128)(2,1)S(1)}, bf16[2,256,128]{2,1,0:T(8,128)(2,1)S(1)}, bf16[256,128]{1,0...) custom-call(s32[3,16]{1,0:T(4,128)} %bitcast.6, ...), custom_call_target="tpu_custom_call" | custom-call | flops 3221225472 | bytes 16777216 | tf_op jit(solution)/shard_map/pallas_call | solution.py:221
  6.6 0.6 %collective-permute-start.3 = (bf16[2,256,128]{2,1,0:T(8,128)(2,1)S(1)}, bf16[2,256,128]{2,1,0:T(8,128)(2,1)S(1)}, u32[]{:S(2)}, u32[]{:S(2)}) collective-permute-start(bf16[2,256,128]{2,1,0:T(8,128)(2,1)S(1)} %get-tuple-element.21), channel_id=1, source_target_pairs={{0,1},{1,0},{2,3},{3,2},{4,5},{5,4},{6,7},{7,6},{8,9},{9,8},{10,11... | collective-permute-start | bytes 393224 | tf_op jit(solution)/shard_map/ppermute | solution.py:219
  7.2 0.1 collective-permute-start.1
  7.3 0.4 %collective-permute-start = (bf16[2,256,128]{2,1,0:T(8,128)(2,1)S(1)}, bf16[2,256,128]{2,1,0:T(8,128)(2,1)S(1)}, u32[]{:S(2)}, u32[]{:S(2)}) collective-permute-start(bf16[2,256,128]{2,1,0:T(8,128)(2,1)S(1)} %get-tuple-element.17), channel_id=1, source_target_pairs={{0,1},{1,0},{2,3},{3,2},{4,5},{5,4},{6,7},{7,6},{8,9},{9,8},{10,11... | collective-permute-start | bytes 393224 | tf_op jit(solution)/shard_map/ppermute | solution.py:219
  7.7 0.5 %collective-permute-done.3 = bf16[2,256,128]{2,1,0:T(8,128)(2,1)S(1)} collective-permute-done((bf16[2,256,128]{2,1,0:T(8,128)(2,1)S(1)}, bf16[2,256,128]{2,1,0:T(8,128)(2,1)S(1)}, u32[]{:S(2)}, u32[]{:S(2)}) %collective-permute-start.3) | collective-permute-done | bytes 131104 | tf_op jit(solution)/shard_map/ppermute | solution.py:219
  8.2 0.7 %collective-permute-start.4 = (bf16[2,256,128]{2,1,0:T(8,128)(2,1)S(1)}, bf16[2,256,128]{2,1,0:T(8,128)(2,1)S(1)}, u32[]{:S(2)}, u32[]{:S(2)}) collective-permute-start(bf16[2,256,128]{2,1,0:T(8,128)(2,1)S(1)} %add_convert_fusion), channel_id=1, source_target_pairs={{2,4},{3,5},{4,2},{5,3},{6,8},{7,9},{8,6},{9,7},{10,12},{11,13},{1... | collective-permute-start | bytes 393224 | tf_op jit(solution)/shard_map/ppermute | solution.py:219
  8.9 0.0 collective-permute-done.1
  8.9 5.7 %collective-permute-start.2 = (bf16[2,256,128]{2,1,0:T(8,128)(2,1)S(1)}, bf16[2,256,128]{2,1,0:T(8,128)(2,1)S(1)}, u32[]{:S(2)}, u32[]{:S(2)}) collective-permute-start(bf16[2,256,128]{2,1,0:T(8,128)(2,1)S(1)} %add_convert_fusion.1), channel_id=1, source_target_pairs={{0,2},{1,3},{2,0},{3,1},{4,6},{5,7},{6,4},{7,5},{8,10},{9,11},{10,... | collective-permute-start | bytes 393224 | tf_op jit(solution)/shard_map/ppermute | solution.py:219
  14.6 0.7 %collective-permute-start.5 = (bf16[256,128]{1,0:T(8,128)(2,1)S(1)}, bf16[256,128]{1,0:T(8,128)(2,1)S(1)}, u32[]{:S(2)}, u32[]{:S(2)}) collective-permute-start(bf16[256,128]{1,0:T(8,128)(2,1)S(1)} %get-tuple-element.22), channel_id=1, source_target_pairs={{1,4},{3,6},{4,1},{5,8},{6,3},{7,10},{8,5},{9,12},{10,7},{11,14},{... | collective-permute-start | bytes 196616 | tf_op jit(solution)/shard_map/ppermute | solution.py:219
  15.3 0.0 copy-done
  15.3 0.3 %shard_map.57.matrix_ref = bf16[128,96]{1,0:T(8,128)(2,1)S(1)} custom-call(f32[2,16,64]{2,1,0:T(8,128)S(1)} %bitcast.4), custom_call_target="tpu_custom_call" | custom-call | flops 10000000 | bytes 32768 | tf_op jit(solution)/shard_map/pallas_call | solution.py:257
  15.6 0.7 %shard_map.56.own_ref = f32[2,256,128]{2,1,0:T(8,128)S(1)} custom-call(bf16[8,2,16,2048]{3,2,1,0:T(8,128)(2,1)S(1)} %get-tuple-element.14.rows, bf16[2,2048,256]{2,1,0:T(8,128)(2,1)S(1)} %get-tuple-element.15.centre, f32[2,256,128]{2,1,0:T(8,128)S(1)} %get-tuple-element.16.own_ref), custom_call_target="tpu_custom_call" | custom-call | flops 536870912 | bytes 1048576 | tf_op jit(solution)/shard_map/pallas_call | solution.py:266
  16.3 0.0 collective-permute-done.5.far_ref
  16.3 0.0 collective-permute-done.mid_ref
  16.3 0.0 collective-permute-done.4.next_ref
  16.4 3.4 %collective-permute-done.2.near_ref = bf16[2,256,128]{2,1,0:T(8,128)(2,1)S(1)} collective-permute-done((bf16[2,256,128]{2,1,0:T(8,128)(2,1)S(1)}, bf16[2,256,128]{2,1,0:T(8,128)(2,1)S(1)}, u32[]{:S(2)}, u32[]{:S(2)}) %collective-permute-start.2) | collective-permute-done | bytes 131104 | tf_op jit(solution)/shard_map/ppermute | solution.py:219
  19.8 1.3 %shard_map.58 = f32[128,8,256]{2,1,0:T(8,128)} custom-call(f32[2,256,128]{2,1,0:T(8,128)S(1)} %shard_map.56.own_ref, bf16[2,256,128]{2,1,0:T(8,128)(2,1)S(1)} %collective-permute-done.mid_ref, bf16[2,256,128]{2,1,0:T(8,128)(2,1)S(1)} %collective-permute-done.2.near_ref, bf16[2,256,128]{2,1,0:T(8,128)(2,1)S(1)} %collective-permute-done.4.next_ref, ...), custom_call_target="tpu_custom_call" | custom-call | flops 100000000 | bytes 2097152 | tf_op jit(solution)/shard_map/pallas_call | solution.py:276
  (2 shorter events, 0.1 us)
Async XLA Ops:
  0.0 15.3 %copy-start = (f32[2,64,16]{1,2,0:T(8,128)S(1)}, f32[2,64,16]{1,2,0:T(8,128)}, u32[]{:S(2)}) copy-start(f32[2,64,16]{1,2,0:T(8,128)} %param.7) | copy-start | bytes 24580
  6.6 1.6 %collective-permute-start.3 = (bf16[2,256,128]{2,1,0:T(8,128)(2,1)S(1)}, bf16[2,256,128]{2,1,0:T(8,128)(2,1)S(1)}, u32[]{:S(2)}, u32[]{:S(2)}) collective-permute-start(bf16[2,256,128]{2,1,0:T(8,128)(2,1)S(1)} %get-tuple-element.21), channel_id=1, source_target_pairs={{0,1},{1,0},{2,3},{3,2},{4,5},{5,4},{6,7},{7,6},{8,9},{9,8},{10,11... | collective-permute-start | bytes 393224 | tf_op jit(solution)/shard_map/ppermute | solution.py:219
  7.2 1.7 %collective-permute-start.1 = (bf16[2,256,128]{2,1,0:T(8,128)(2,1)S(1)}, bf16[2,256,128]{2,1,0:T(8,128)(2,1)S(1)}, u32[]{:S(2)}, u32[]{:S(2)}) collective-permute-start(bf16[2,256,128]{2,1,0:T(8,128)(2,1)S(1)} %get-tuple-element.19), channel_id=1, source_target_pairs={{0,1},{1,0},{2,3},{3,2},{4,5},{5,4},{6,7},{7,6},{8,9},{9,8},{10,11... | collective-permute-start | bytes 393224 | tf_op jit(solution)/shard_map/ppermute | solution.py:219
  7.3 9.1 %collective-permute-start = (bf16[2,256,128]{2,1,0:T(8,128)(2,1)S(1)}, bf16[2,256,128]{2,1,0:T(8,128)(2,1)S(1)}, u32[]{:S(2)}, u32[]{:S(2)}) collective-permute-start(bf16[2,256,128]{2,1,0:T(8,128)(2,1)S(1)} %get-tuple-element.17), channel_id=1, source_target_pairs={{0,1},{1,0},{2,3},{3,2},{4,5},{5,4},{6,7},{7,6},{8,9},{9,8},{10,11... | collective-permute-start | bytes 393224 | tf_op jit(solution)/shard_map/ppermute | solution.py:219
  8.2 8.1 %collective-permute-start.4 = (bf16[2,256,128]{2,1,0:T(8,128)(2,1)S(1)}, bf16[2,256,128]{2,1,0:T(8,128)(2,1)S(1)}, u32[]{:S(2)}, u32[]{:S(2)}) collective-permute-start(bf16[2,256,128]{2,1,0:T(8,128)(2,1)S(1)} %add_convert_fusion), channel_id=1, source_target_pairs={{2,4},{3,5},{4,2},{5,3},{6,8},{7,9},{8,6},{9,7},{10,12},{11,13},{1... | collective-permute-start | bytes 393224 | tf_op jit(solution)/shard_map/ppermute | solution.py:219
  8.9 10.8 %collective-permute-start.2 = (bf16[2,256,128]{2,1,0:T(8,128)(2,1)S(1)}, bf16[2,256,128]{2,1,0:T(8,128)(2,1)S(1)}, u32[]{:S(2)}, u32[]{:S(2)}) collective-permute-start(bf16[2,256,128]{2,1,0:T(8,128)(2,1)S(1)} %add_convert_fusion.1), channel_id=1, source_target_pairs={{0,2},{1,3},{2,0},{3,1},{4,6},{5,7},{6,4},{7,5},{8,10},{9,11},{10,... | collective-permute-start | bytes 393224 | tf_op jit(solution)/shard_map/ppermute | solution.py:219
  14.6 1.7 %collective-permute-start.5 = (bf16[256,128]{1,0:T(8,128)(2,1)S(1)}, bf16[256,128]{1,0:T(8,128)(2,1)S(1)}, u32[]{:S(2)}, u32[]{:S(2)}) collective-permute-start(bf16[256,128]{1,0:T(8,128)(2,1)S(1)} %get-tuple-element.22), channel_id=1, source_target_pairs={{1,4},{3,6},{4,1},{5,8},{6,3},{7,10},{8,5},{9,12},{10,7},{11,14},{... | collective-permute-start | bytes 196616 | tf_op jit(solution)/shard_map/ppermute | solution.py:219

commit v3 on v2

--- a/solution.py
+++ b/solution.py
@@ -105,9 +105,9 @@
     first = 4 * (1 - odd)
     upward = 8 * (1 - lax.rem(block // 2, 2))
     for k in range(2):
-        swap_ref[k] = slots[first + upward + k].astype(BF16)
+        swap_ref[k] = slots[2 + upward + k].astype(BF16)
         cross_ref[k] = slots[first + 8 - upward + k].astype(BF16)
-        near_ref[k] = slots[2 + upward + k]
+        near_ref[k] = slots[first + upward + k]
         next_ref[k] = slots[10 - upward + k]
         mid_ref[k] = slots[first + 4 + k].astype(BF16)
         own_ref[k] = slots[6 + k]
@@ -251,7 +251,7 @@
     next_sum = (nxt + crossed.astype(F32)).astype(BF16)
     near_sum = (near + swapped.astype(F32)).astype(BF16)
     next_got = send(next_sum, lambda i: i + 2 if i // 2 % 2 else i - 2)
-    near_got = send(near_sum, lambda i: i - 2 if i // 2 % 2 else i + 2)
+    near_got = send(near_sum, lambda i: i ^ 3)
     mid_got = send(mid, lambda i: i ^ 1)
 
     matrix = pl.pallas_call(

time: 21.2 us -> 21.3 us (level)
  the two profiles are of different devices: /device:TPU:0 before, /device:TPU:1 now
where the time goes in v3:
time: 21.3 us; the launch traced here: 21.2 us
  starting transfers between devices  9.71 us (46%)
  Pallas kernels  8.96 us (42%)
  waiting for transfers between devices  2.36 us (11%)
    ppermute x6, starting transfers between devices, send(): lax.ppermute(x, 'track', [(i, to(i)) for i in range(peers) if 0 <= to(i)...  9.71 us
    pallas_call x1, Pallas kernels, body(): pl.pallas_call(backproject, out_shape=(halves(2, BF16), halves(2, BF16),...  6.62 us
    ppermute x6, waiting for transfers between devices, send(): lax.ppermute(x, 'track', [(i, to(i)) for i in range(peers) if 0 <= to(i)...  2.36 us
    pallas_call x1, Pallas kernels, body(): pl.pallas_call(focus, out_shape=jax.ShapeDtypeStruct((2 * heights, tiles,...  1.34 us
    pallas_call x1, Pallas kernels, body(): pl.pallas_call(finish_own, out_shape=halves(2, F32), in_specs=[VMEM_SPEC]...  0.71 us
  transfers between devices with their start and end apart: 6, of which 2 were waited for; matrix products, arithmetic and copies ran while one was open for 0% of the time, Pallas kernels for 5%

profile of v3, /device:TPU:1, one launch (start us, length us, event | category | flops | bytes accessed | tf_op | source)
XLA Modules:
  0.0 21.2 jit_solution(14123928052777878537)
XLA Ops:
  0.0 0.0 copy-start
  0.0 6.6 %shard_map.55 = (bf16[2,256,128]{2,1,0:T(8,128)(2,1)S(1)}, bf16[2,256,128]{2,1,0:T(8,128)(2,1)S(1)}, bf16[2,256,128]{2,1,0:T(8,128)(2,1)S(1)}, bf16[256,128]{1,0...) custom-call(s32[3,16]{1,0:T(4,128)} %bitcast.6, ...), custom_call_target="tpu_custom_call" | custom-call | flops 3221225472 | bytes 16777216 | tf_op jit(solution)/shard_map/pallas_call | solution.py:221
  6.6 0.1 collective-permute-start.3
  6.7 0.5 %collective-permute-start.1 = (bf16[2,256,128]{2,1,0:T(8,128)(2,1)S(1)}, bf16[2,256,128]{2,1,0:T(8,128)(2,1)S(1)}, u32[]{:S(2)}, u32[]{:S(2)}) collective-permute-start(bf16[2,256,128]{2,1,0:T(8,128)(2,1)S(1)} %get-tuple-element.19), channel_id=1, source_target_pairs={{0,1},{1,0},{2,3},{3,2},{4,5},{5,4},{6,7},{7,6},{8,9},{9,8},{10,11... | collective-permute-start | bytes 393224 | tf_op jit(solution)/shard_map/ppermute | solution.py:219
  7.2 0.1 collective-permute-start
  7.3 0.8 %collective-permute-done.3 = bf16[2,256,128]{2,1,0:T(8,128)(2,1)S(1)} collective-permute-done((bf16[2,256,128]{2,1,0:T(8,128)(2,1)S(1)}, bf16[2,256,128]{2,1,0:T(8,128)(2,1)S(1)}, u32[]{:S(2)}, u32[]{:S(2)}) %collective-permute-start.3) | collective-permute-done | bytes 131104 | tf_op jit(solution)/shard_map/ppermute | solution.py:219
  8.1 0.7 %collective-permute-start.4 = (bf16[2,256,128]{2,1,0:T(8,128)(2,1)S(1)}, bf16[2,256,128]{2,1,0:T(8,128)(2,1)S(1)}, u32[]{:S(2)}, u32[]{:S(2)}) collective-permute-start(bf16[2,256,128]{2,1,0:T(8,128)(2,1)S(1)} %add_convert_fusion), channel_id=1, source_target_pairs={{2,4},{3,5},{4,2},{5,3},{6,8},{7,9},{8,6},{9,7},{10,12},{11,13},{1... | collective-permute-start | bytes 393224 | tf_op jit(solution)/shard_map/ppermute | solution.py:219
  8.8 0.0 collective-permute-done.1
  8.8 5.4 %collective-permute-start.2 = (bf16[2,256,128]{2,1,0:T(8,128)(2,1)S(1)}, bf16[2,256,128]{2,1,0:T(8,128)(2,1)S(1)}, u32[]{:S(2)}, u32[]{:S(2)}) collective-permute-start(bf16[2,256,128]{2,1,0:T(8,128)(2,1)S(1)} %add_convert_fusion.1), channel_id=1, source_target_pairs={{0,3},{1,2},{2,1},{3,0},{4,7},{5,6},{6,5},{7,4},{8,11},{9,10},{10,... | collective-permute-start | bytes 393224 | tf_op jit(solution)/shard_map/ppermute | solution.py:219
  14.3 2.9 %collective-permute-start.5 = (bf16[256,128]{1,0:T(8,128)(2,1)S(1)}, bf16[256,128]{1,0:T(8,128)(2,1)S(1)}, u32[]{:S(2)}, u32[]{:S(2)}) collective-permute-start(bf16[256,128]{1,0:T(8,128)(2,1)S(1)} %get-tuple-element.22), channel_id=1, source_target_pairs={{1,4},{3,6},{4,1},{5,8},{6,3},{7,10},{8,5},{9,12},{10,7},{11,14},{... | collective-permute-start | bytes 196616 | tf_op jit(solution)/shard_map/ppermute | solution.py:219
  17.2 0.0 copy-done
  17.2 0.3 %shard_map.57.matrix_ref = bf16[128,96]{1,0:T(8,128)(2,1)S(1)} custom-call(f32[2,16,64]{2,1,0:T(8,128)S(1)} %bitcast.4), custom_call_target="tpu_custom_call" | custom-call | flops 10000000 | bytes 32768 | tf_op jit(solution)/shard_map/pallas_call | solution.py:257
  17.5 0.7 %shard_map.56.own_ref = f32[2,256,128]{2,1,0:T(8,128)S(1)} custom-call(bf16[8,2,16,2048]{3,2,1,0:T(8,128)(2,1)S(1)} %get-tuple-element.14.rows, bf16[2,2048,256]{2,1,0:T(8,128)(2,1)S(1)} %get-tuple-element.15.centre, f32[2,256,128]{2,1,0:T(8,128)S(1)} %get-tuple-element.16.own_ref), custom_call_target="tpu_custom_call" | custom-call | flops 536870912 | bytes 1048576 | tf_op jit(solution)/shard_map/pallas_call | solution.py:266
  18.2 1.6 %collective-permute-done.5.far_ref = bf16[256,128]{1,0:T(8,128)(2,1)S(1)} collective-permute-done((bf16[256,128]{1,0:T(8,128)(2,1)S(1)}, bf16[256,128]{1,0:T(8,128)(2,1)S(1)}, u32[]{:S(2)}, u32[]{:S(2)}) %collective-permute-start.5) | collective-permute-done | bytes 65568 | tf_op jit(solution)/shard_map/ppermute | solution.py:219
  19.8 0.0 collective-permute-done.mid_ref
  19.8 0.0 collective-permute-done.4.next_ref
  19.8 0.0 collective-permute-done.2.near_ref
  19.8 1.3 %shard_map.58 = f32[128,8,256]{2,1,0:T(8,128)} custom-call(f32[2,256,128]{2,1,0:T(8,128)S(1)} %shard_map.56.own_ref, bf16[2,256,128]{2,1,0:T(8,128)(2,1)S(1)} %collective-permute-done.mid_ref, bf16[2,256,128]{2,1,0:T(8,128)(2,1)S(1)} %collective-permute-done.2.near_ref, bf16[2,256,128]{2,1,0:T(8,128)(2,1)S(1)} %collective-permute-done.4.next_ref, ...), custom_call_target="tpu_custom_call" | custom-call | flops 100000000 | bytes 2097152 | tf_op jit(solution)/shard_map/pallas_call | solution.py:276
  (2 shorter events, 0.1 us)
Async XLA Ops:
  0.0 17.2 %copy-start = (f32[2,64,16]{1,2,0:T(8,128)S(1)}, f32[2,64,16]{1,2,0:T(8,128)}, u32[]{:S(2)}) copy-start(f32[2,64,16]{1,2,0:T(8,128)} %param.7) | copy-start | bytes 24580
  6.6 1.4 %collective-permute-start.3 = (bf16[2,256,128]{2,1,0:T(8,128)(2,1)S(1)}, bf16[2,256,128]{2,1,0:T(8,128)(2,1)S(1)}, u32[]{:S(2)}, u32[]{:S(2)}) collective-permute-start(bf16[2,256,128]{2,1,0:T(8,128)(2,1)S(1)} %get-tuple-element.21), channel_id=1, source_target_pairs={{0,1},{1,0},{2,3},{3,2},{4,5},{5,4},{6,7},{7,6},{8,9},{9,8},{10,11... | collective-permute-start | bytes 393224 | tf_op jit(solution)/shard_map/ppermute | solution.py:219
  6.7 2.1 %collective-permute-start.1 = (bf16[2,256,128]{2,1,0:T(8,128)(2,1)S(1)}, bf16[2,256,128]{2,1,0:T(8,128)(2,1)S(1)}, u32[]{:S(2)}, u32[]{:S(2)}) collective-permute-start(bf16[2,256,128]{2,1,0:T(8,128)(2,1)S(1)} %get-tuple-element.19), channel_id=1, source_target_pairs={{0,1},{1,0},{2,3},{3,2},{4,5},{5,4},{6,7},{7,6},{8,9},{9,8},{10,11... | collective-permute-start | bytes 393224 | tf_op jit(solution)/shard_map/ppermute | solution.py:219
  7.2 12.6 %collective-permute-start = (bf16[2,256,128]{2,1,0:T(8,128)(2,1)S(1)}, bf16[2,256,128]{2,1,0:T(8,128)(2,1)S(1)}, u32[]{:S(2)}, u32[]{:S(2)}) collective-permute-start(bf16[2,256,128]{2,1,0:T(8,128)(2,1)S(1)} %get-tuple-element.17), channel_id=1, source_target_pairs={{0,1},{1,0},{2,3},{3,2},{4,5},{5,4},{6,7},{7,6},{8,9},{9,8},{10,11... | collective-permute-start | bytes 393224 | tf_op jit(solution)/shard_map/ppermute | solution.py:219
  8.1 11.8 %collective-permute-start.4 = (bf16[2,256,128]{2,1,0:T(8,128)(2,1)S(1)}, bf16[2,256,128]{2,1,0:T(8,128)(2,1)S(1)}, u32[]{:S(2)}, u32[]{:S(2)}) collective-permute-start(bf16[2,256,128]{2,1,0:T(8,128)(2,1)S(1)} %add_convert_fusion), channel_id=1, source_target_pairs={{2,4},{3,5},{4,2},{5,3},{6,8},{7,9},{8,6},{9,7},{10,12},{11,13},{1... | collective-permute-start | bytes 393224 | tf_op jit(solution)/shard_map/ppermute | solution.py:219
  8.8 11.0 %collective-permute-start.2 = (bf16[2,256,128]{2,1,0:T(8,128)(2,1)S(1)}, bf16[2,256,128]{2,1,0:T(8,128)(2,1)S(1)}, u32[]{:S(2)}, u32[]{:S(2)}) collective-permute-start(bf16[2,256,128]{2,1,0:T(8,128)(2,1)S(1)} %add_convert_fusion.1), channel_id=1, source_target_pairs={{0,3},{1,2},{2,1},{3,0},{4,7},{5,6},{6,5},{7,4},{8,11},{9,10},{10,... | collective-permute-start | bytes 393224 | tf_op jit(solution)/shard_map/ppermute | solution.py:219
  14.3 5.6 %collective-permute-start.5 = (bf16[256,128]{1,0:T(8,128)(2,1)S(1)}, bf16[256,128]{1,0:T(8,128)(2,1)S(1)}, u32[]{:S(2)}, u32[]{:S(2)}) collective-permute-start(bf16[256,128]{1,0:T(8,128)(2,1)S(1)} %get-tuple-element.22), channel_id=1, source_target_pairs={{1,4},{3,6},{4,1},{5,8},{6,3},{7,10},{8,5},{9,12},{10,7},{11,14},{... | collective-permute-start | bytes 196616 | tf_op jit(solution)/shard_map/ppermute | solution.py:219

commit v4 on v3

--- a/solution.py
+++ b/solution.py
@@ -116,7 +116,7 @@
     last.wait()
 
 
-def finish_own(rows, centre, own_ref, out_ref):
+def finish_own(rows, centre, own_ref, near_ref, out_ref):
     tiles, _, tracks, span = rows.shape
     cols = centre.shape[2]
     half = cols // 2
@@ -129,7 +129,8 @@
         part = part.reshape(many, cols).astype(BF16).astype(F32)
         at = slice(k * many, (k + 1) * many)
         for n in range(2):
-            out_ref[n, at] = own_ref[n, at] + part[:, n * half : (n + 1) * half]
+            held = own_ref[n, at] + near_ref[n, at].astype(F32)
+            out_ref[n, at] = held + part[:, n * half : (n + 1) * half]
 
 
 def fold(steer_ref, out_ref):
@@ -159,13 +160,13 @@
     out_ref[heights:] = imag.astype(BF16)
 
 
-def focus(own_ref, mid_ref, near_ref, next_ref, far_ref, matrix_ref, out_hbm, pieces, out, sem):
+def focus(own_ref, mid_ref, next_ref, far_ref, matrix_ref, out_hbm, pieces, out, sem):
     _, lines, tiles, half = out.shape
     tracks = own_ref.shape[1] // (2 * tiles)
     odd = lax.rem(lax.axis_index("track"), 2)
     for k in range(2):
         total = own_ref[k] + mid_ref[k].astype(F32)
-        total += near_ref[k].astype(F32) + next_ref[k].astype(F32)
+        total += next_ref[k].astype(F32)
         total += jnp.where(odd == k, far_ref[...].astype(F32), 0.0)
         high = total.astype(BF16)
         low = (total - high.astype(F32)).astype(BF16)
@@ -266,17 +267,17 @@
     own = pl.pallas_call(
         finish_own,
         out_shape=halves(2, F32),
-        in_specs=[VMEM_SPEC] * 3,
+        in_specs=[VMEM_SPEC] * 4,
         out_specs=VMEM_SPEC,
         compiler_params=pltpu.CompilerParams(vmem_limit_bytes=12 << 20),
         cost_estimate=pl.CostEstimate(flops=2 * rows * span * footprint, bytes_accessed=1 << 20, transcendentals=0),
-    )(*(placed_in(x, "VMEM") for x in (picked, centre, own)))
+    )(*(placed_in(x, "VMEM") for x in (picked, centre, own, near_got)))
 
     steps = 2
     volume = pl.pallas_call(
         focus,
         out_shape=jax.ShapeDtypeStruct((2 * heights, tiles, 2 * half), F32),
-        in_specs=[VMEM_SPEC] * 6,
+        in_specs=[VMEM_SPEC] * 5,
         out_specs=HBM_SPEC,
         scratch_shapes=[
             pltpu.VMEM((tiles, 6 * tracks, 2 * half), BF16),
@@ -285,7 +286,7 @@
         ],
         compiler_params=pltpu.CompilerParams(vmem_limit_bytes=12 << 20),
         cost_estimate=pl.CostEstimate(flops=100_000_000, bytes_accessed=2 << 20, transcendentals=0),
-    )(*(placed_in(x, "VMEM") for x in (own, mid_got, near_got, next_got, far_got, matrix)))
+    )(*(placed_in(x, "VMEM") for x in (own, mid_got, next_got, far_got, matrix)))
     return volume.reshape(2, heights, tiles, 2 * half)
 
 

time: 21.3 us -> 20.2 us (0.948)
  the two profiles are of different devices: /device:TPU:1 before, /device:TPU:15 now
where the time goes in v4:
time: 20.2 us; the launch traced here: 20.1 us
  starting transfers between devices  9.29 us (46%)
  Pallas kernels  8.92 us (44%)
  waiting for transfers between devices  1.72 us (9%)
    ppermute x6, starting transfers between devices, send(): lax.ppermute(x, 'track', [(i, to(i)) for i in range(peers) if 0 <= to(i)...  9.29 us
    pallas_call x1, Pallas kernels, body(): pl.pallas_call(backproject, out_shape=(halves(2, BF16), halves(2, BF16),...  6.62 us
    ppermute x6, waiting for transfers between devices, send(): lax.ppermute(x, 'track', [(i, to(i)) for i in range(peers) if 0 <= to(i)...  1.72 us
    pallas_call x1, Pallas kernels, body(): pl.pallas_call(focus, out_shape=jax.ShapeDtypeStruct((2 * heights, tiles,...  1.3 us
    pallas_call x1, Pallas kernels, body(): pl.pallas_call(finish_own, out_shape=halves(2, F32), in_specs=[VMEM_SPEC]...  0.71 us
  transfers between devices with their start and end apart: 6, of which 2 were waited for; matrix products, arithmetic and copies ran while one was open for 0% of the time, Pallas kernels for 5%

profile of v4, /device:TPU:15, one launch (start us, length us, event | category | flops | bytes accessed | tf_op | source)
XLA Modules:
  0.0 20.1 jit_solution(14671748450278717788)
XLA Ops:
  0.0 0.0 copy-start
  0.0 6.6 %shard_map.55 = (bf16[2,256,128]{2,1,0:T(8,128)(2,1)S(1)}, bf16[2,256,128]{2,1,0:T(8,128)(2,1)S(1)}, bf16[2,256,128]{2,1,0:T(8,128)(2,1)S(1)}, bf16[256,128]{1,0...) custom-call(s32[3,16]{1,0:T(4,128)} %bitcast.6, ...), custom_call_target="tpu_custom_call" | custom-call | flops 3221225472 | bytes 16777216 | tf_op jit(solution)/shard_map/pallas_call | solution.py:222
  6.6 0.8 %collective-permute-start = (bf16[2,256,128]{2,1,0:T(8,128)(2,1)S(1)}, bf16[2,256,128]{2,1,0:T(8,128)(2,1)S(1)}, u32[]{:S(2)}, u32[]{:S(2)}) collective-permute-start(bf16[2,256,128]{2,1,0:T(8,128)(2,1)S(1)} %get-tuple-element.18), channel_id=1, source_target_pairs={{0,1},{1,0},{2,3},{3,2},{4,5},{5,4},{6,7},{7,6},{8,9},{9,8},{10,11... | collective-permute-start | bytes 393224 | tf_op jit(solution)/shard_map/ppermute | solution.py:220
  7.4 0.1 collective-permute-start.3
  7.5 0.4 %collective-permute-start.2 = (bf16[2,256,128]{2,1,0:T(8,128)(2,1)S(1)}, bf16[2,256,128]{2,1,0:T(8,128)(2,1)S(1)}, u32[]{:S(2)}, u32[]{:S(2)}) collective-permute-start(bf16[2,256,128]{2,1,0:T(8,128)(2,1)S(1)} %get-tuple-element.19), channel_id=1, source_target_pairs={{0,1},{1,0},{2,3},{3,2},{4,5},{5,4},{6,7},{7,6},{8,9},{9,8},{10,11... | collective-permute-start | bytes 393224 | tf_op jit(solution)/shard_map/ppermute | solution.py:220
  7.9 0.5 %collective-permute-done = bf16[2,256,128]{2,1,0:T(8,128)(2,1)S(1)} collective-permute-done((bf16[2,256,128]{2,1,0:T(8,128)(2,1)S(1)}, bf16[2,256,128]{2,1,0:T(8,128)(2,1)S(1)}, u32[]{:S(2)}, u32[]{:S(2)}) %collective-permute-start) | collective-permute-done | bytes 131104 | tf_op jit(solution)/shard_map/ppermute | solution.py:220
  8.4 0.5 %collective-permute-start.1 = (bf16[2,256,128]{2,1,0:T(8,128)(2,1)S(1)}, bf16[2,256,128]{2,1,0:T(8,128)(2,1)S(1)}, u32[]{:S(2)}, u32[]{:S(2)}) collective-permute-start(bf16[2,256,128]{2,1,0:T(8,128)(2,1)S(1)} %add_convert_fusion.1), channel_id=1, source_target_pairs={{0,3},{1,2},{2,1},{3,0},{4,7},{5,6},{6,5},{7,4},{8,11},{9,10},{10,... | collective-permute-start | bytes 393224 | tf_op jit(solution)/shard_map/ppermute | solution.py:220
  8.9 0.0 collective-permute-done.3
  9.0 4.2 %collective-permute-start.4 = (bf16[2,256,128]{2,1,0:T(8,128)(2,1)S(1)}, bf16[2,256,128]{2,1,0:T(8,128)(2,1)S(1)}, u32[]{:S(2)}, u32[]{:S(2)}) collective-permute-start(bf16[2,256,128]{2,1,0:T(8,128)(2,1)S(1)} %add_convert_fusion), channel_id=1, source_target_pairs={{2,4},{3,5},{4,2},{5,3},{6,8},{7,9},{8,6},{9,7},{10,12},{11,13},{1... | collective-permute-start | bytes 393224 | tf_op jit(solution)/shard_map/ppermute | solution.py:220
  13.1 3.3 %collective-permute-start.5 = (bf16[256,128]{1,0:T(8,128)(2,1)S(1)}, bf16[256,128]{1,0:T(8,128)(2,1)S(1)}, u32[]{:S(2)}, u32[]{:S(2)}) collective-permute-start(bf16[256,128]{1,0:T(8,128)(2,1)S(1)} %get-tuple-element.22), channel_id=1, source_target_pairs={{1,4},{3,6},{4,1},{5,8},{6,3},{7,10},{8,5},{9,12},{10,7},{11,14},{... | collective-permute-start | bytes 196616 | tf_op jit(solution)/shard_map/ppermute | solution.py:220
  16.5 0.0 copy-done
  16.5 0.3 %shard_map.57.matrix_ref = bf16[128,96]{1,0:T(8,128)(2,1)S(1)} custom-call(f32[2,16,64]{2,1,0:T(8,128)S(1)} %bitcast.4), custom_call_target="tpu_custom_call" | custom-call | flops 10000000 | bytes 32768 | tf_op jit(solution)/shard_map/pallas_call | solution.py:258
  16.8 0.0 collective-permute-done.1.near_ref
  16.8 0.7 %shard_map.56.own_ref = f32[2,256,128]{2,1,0:T(8,128)S(1)} custom-call(bf16[8,2,16,2048]{3,2,1,0:T(8,128)(2,1)S(1)} %get-tuple-element.14.rows, bf16[2,2048,256]{2,1,0:T(8,128)(2,1)S(1)} %get-tuple-element.15.centre, f32[2,256,128]{2,1,0:T(8,128)S(1)} %get-tuple-element.16.own_ref, bf16[2,256,128]{2,1,0:T(8,128)(2,1)S(1)} %collective-permute-done.1.near_ref), custom_call_target="tpu_custom_call" | custom-call | flops 536870912 | bytes 1048576 | tf_op jit(solution)/shard_map/pallas_call | solution.py:267
  17.5 1.2 %collective-permute-done.5.far_ref = bf16[256,128]{1,0:T(8,128)(2,1)S(1)} collective-permute-done((bf16[256,128]{1,0:T(8,128)(2,1)S(1)}, bf16[256,128]{1,0:T(8,128)(2,1)S(1)}, u32[]{:S(2)}, u32[]{:S(2)}) %collective-permute-start.5) | collective-permute-done | bytes 65568 | tf_op jit(solution)/shard_map/ppermute | solution.py:220
  18.8 0.0 collective-permute-done.2.mid_ref
  18.8 0.0 collective-permute-done.4.next_ref
  18.8 1.3 %shard_map.58 = f32[128,8,256]{2,1,0:T(8,128)} custom-call(f32[2,256,128]{2,1,0:T(8,128)S(1)} %shard_map.56.own_ref, bf16[2,256,128]{2,1,0:T(8,128)(2,1)S(1)} %collective-permute-done.2.mid_ref, bf16[2,256,128]{2,1,0:T(8,128)(2,1)S(1)} %collective-permute-done.4.next_ref, bf16[256,128]{1,0:T(8,128)(2,1)S(1)} %collective-permute-done.5.far_ref, ...), custom_call_target="tpu_custom_call" | custom-call | flops 100000000 | bytes 2097152 | tf_op jit(solution)/shard_map/pallas_call | solution.py:277
  (2 shorter events, 0.1 us)
Async XLA Ops:
  0.0 16.5 %copy-start = (f32[2,64,16]{1,2,0:T(8,128)S(1)}, f32[2,64,16]{1,2,0:T(8,128)}, u32[]{:S(2)}) copy-start(f32[2,64,16]{1,2,0:T(8,128)} %param.7) | copy-start | bytes 24580
  6.6 1.8 %collective-permute-start = (bf16[2,256,128]{2,1,0:T(8,128)(2,1)S(1)}, bf16[2,256,128]{2,1,0:T(8,128)(2,1)S(1)}, u32[]{:S(2)}, u32[]{:S(2)}) collective-permute-start(bf16[2,256,128]{2,1,0:T(8,128)(2,1)S(1)} %get-tuple-element.18), channel_id=1, source_target_pairs={{0,1},{1,0},{2,3},{3,2},{4,5},{5,4},{6,7},{7,6},{8,9},{9,8},{10,11... | collective-permute-start | bytes 393224 | tf_op jit(solution)/shard_map/ppermute | solution.py:220
  7.4 1.5 %collective-permute-start.3 = (bf16[2,256,128]{2,1,0:T(8,128)(2,1)S(1)}, bf16[2,256,128]{2,1,0:T(8,128)(2,1)S(1)}, u32[]{:S(2)}, u32[]{:S(2)}) collective-permute-start(bf16[2,256,128]{2,1,0:T(8,128)(2,1)S(1)} %get-tuple-element.21), channel_id=1, source_target_pairs={{0,1},{1,0},{2,3},{3,2},{4,5},{5,4},{6,7},{7,6},{8,9},{9,8},{10,11... | collective-permute-start | bytes 393224 | tf_op jit(solution)/shard_map/ppermute | solution.py:220
  7.5 11.3 %collective-permute-start.2 = (bf16[2,256,128]{2,1,0:T(8,128)(2,1)S(1)}, bf16[2,256,128]{2,1,0:T(8,128)(2,1)S(1)}, u32[]{:S(2)}, u32[]{:S(2)}) collective-permute-start(bf16[2,256,128]{2,1,0:T(8,128)(2,1)S(1)} %get-tuple-element.19), channel_id=1, source_target_pairs={{0,1},{1,0},{2,3},{3,2},{4,5},{5,4},{6,7},{7,6},{8,9},{9,8},{10,11... | collective-permute-start | bytes 393224 | tf_op jit(solution)/shard_map/ppermute | solution.py:220
  8.4 8.4 %collective-permute-start.1 = (bf16[2,256,128]{2,1,0:T(8,128)(2,1)S(1)}, bf16[2,256,128]{2,1,0:T(8,128)(2,1)S(1)}, u32[]{:S(2)}, u32[]{:S(2)}) collective-permute-start(bf16[2,256,128]{2,1,0:T(8,128)(2,1)S(1)} %add_convert_fusion.1), channel_id=1, source_target_pairs={{0,3},{1,2},{2,1},{3,0},{4,7},{5,6},{6,5},{7,4},{8,11},{9,10},{10,... | collective-permute-start | bytes 393224 | tf_op jit(solution)/shard_map/ppermute | solution.py:220
  9.0 9.8 %collective-permute-start.4 = (bf16[2,256,128]{2,1,0:T(8,128)(2,1)S(1)}, bf16[2,256,128]{2,1,0:T(8,128)(2,1)S(1)}, u32[]{:S(2)}, u32[]{:S(2)}) collective-permute-start(bf16[2,256,128]{2,1,0:T(8,128)(2,1)S(1)} %add_convert_fusion), channel_id=1, source_target_pairs={{2,4},{3,5},{4,2},{5,3},{6,8},{7,9},{8,6},{9,7},{10,12},{11,13},{1... | collective-permute-start | bytes 393224 | tf_op jit(solution)/shard_map/ppermute | solution.py:220
  13.1 5.6 %collective-permute-start.5 = (bf16[256,128]{1,0:T(8,128)(2,1)S(1)}, bf16[256,128]{1,0:T(8,128)(2,1)S(1)}, u32[]{:S(2)}, u32[]{:S(2)}) collective-permute-start(bf16[256,128]{1,0:T(8,128)(2,1)S(1)} %get-tuple-element.22), channel_id=1, source_target_pairs={{1,4},{3,6},{4,1},{5,8},{6,3},{7,10},{8,5},{9,12},{10,7},{11,14},{... | collective-permute-start | bytes 196616 | tf_op jit(solution)/shard_map/ppermute | solution.py:220

commit v5 on v4

--- a/solution.py
+++ b/solution.py
@@ -164,6 +164,7 @@
     _, lines, tiles, half = out.shape
     tracks = own_ref.shape[1] // (2 * tiles)
     odd = lax.rem(lax.axis_index("track"), 2)
+    copies = []
     for k in range(2):
         total = own_ref[k] + mid_ref[k].astype(F32)
         total += next_ref[k].astype(F32)
@@ -178,23 +179,14 @@
                     to = (2 * place + part) * tracks
                     pieces[tile, to : to + tracks, cols] = piece[start : start + tracks]
 
-    steps = sem.shape[0]
-    count = lines // steps
-    copies = []
-    for i in range(steps):
-        matrix = matrix_ref[i * count : (i + 1) * count]
+        flat = out.at[k].reshape(lines * tiles, half)
         for tile in range(tiles):
-            sums = jnp.dot(matrix, pieces[tile], preferred_element_type=F32)
-            for k in range(2):
-                flat = out.at[k].reshape(lines * tiles, half)
-                flat[pl.ds(i * count * tiles + tile, count, stride=tiles)] = sums[:, k * half : (k + 1) * half]
-        here = pl.ds(i * count, count)
-        for k in range(2):
-            copy = pltpu.make_async_copy(
-                out.at[k, here], out_hbm.at[here, :, k * half : (k + 1) * half], sem.at[i, k]
+            flat[pl.ds(tile, lines, stride=tiles)] = jnp.dot(
+                matrix_ref[...], pieces[tile, :, cols], preferred_element_type=F32
             )
-            copy.start()
-            copies.append(copy)
+        copy = pltpu.make_async_copy(out.at[k], out_hbm.at[:, :, cols], sem.at[k])
+        copy.start()
+        copies.append(copy)
     for copy in copies:
         copy.wait()
 
@@ -273,7 +265,6 @@
         cost_estimate=pl.CostEstimate(flops=2 * rows * span * footprint, bytes_accessed=1 << 20, transcendentals=0),
     )(*(placed_in(x, "VMEM") for x in (picked, centre, own, near_got)))
 
-    steps = 2
     volume = pl.pallas_call(
         focus,
         out_shape=jax.ShapeDtypeStruct((2 * heights, tiles, 2 * half), F32),
@@ -282,7 +273,7 @@
         scratch_shapes=[
             pltpu.VMEM((tiles, 6 * tracks, 2 * half), BF16),
             pltpu.VMEM((2, 2 * heights, tiles, half), F32),
-            pltpu.SemaphoreType.DMA((steps, 2)),
+            pltpu.SemaphoreType.DMA((2,)),
         ],
         compiler_params=pltpu.CompilerParams(vmem_limit_bytes=12 << 20),
         cost_estimate=pl.CostEstimate(flops=100_000_000, bytes_accessed=2 << 20, transcendentals=0),

time: 20.2 us -> 20.2 us (level)
  no operation moved by 1% of the time
where the time goes in v5:
time: 20.2 us; the launch traced here: 20 us
  starting transfers between devices  9.29 us (46%)
  Pallas kernels  8.88 us (44%)
  waiting for transfers between devices  1.72 us (9%)
    ppermute x6, starting transfers between devices, send(): lax.ppermute(x, 'track', [(i, to(i)) for i in range(peers) if 0 <= to(i)...  9.29 us
    pallas_call x1, Pallas kernels, body(): pl.pallas_call(backproject, out_shape=(halves(2, BF16), halves(2, BF16),...  6.62 us
    ppermute x6, waiting for transfers between devices, send(): lax.ppermute(x, 'track', [(i, to(i)) for i in range(peers) if 0 <= to(i)...  1.72 us
    pallas_call x1, Pallas kernels, body(): pl.pallas_call(focus, out_shape=jax.ShapeDtypeStruct((2 * heights, tiles,...  1.26 us
    pallas_call x1, Pallas kernels, body(): pl.pallas_call(finish_own, out_shape=halves(2, F32), in_specs=[VMEM_SPEC]...  0.71 us
  transfers between devices with their start and end apart: 6, of which 2 were waited for; matrix products, arithmetic and copies ran while one was open for 0% of the time, Pallas kernels for 5%

profile of v5, /device:TPU:15, one launch (start us, length us, event | category | flops | bytes accessed | tf_op | source)
XLA Modules:
  0.0 20.0 jit_solution(17102987458641679082)
XLA Ops:
  0.0 0.0 copy-start
  0.0 6.6 %shard_map.55 = (bf16[2,256,128]{2,1,0:T(8,128)(2,1)S(1)}, bf16[2,256,128]{2,1,0:T(8,128)(2,1)S(1)}, bf16[2,256,128]{2,1,0:T(8,128)(2,1)S(1)}, bf16[256,128]{1,0...) custom-call(s32[3,16]{1,0:T(4,128)} %bitcast.6, ...), custom_call_target="tpu_custom_call" | custom-call | flops 3221225472 | bytes 16777216 | tf_op jit(solution)/shard_map/pallas_call | solution.py:214
  6.6 0.8 %collective-permute-start = (bf16[2,256,128]{2,1,0:T(8,128)(2,1)S(1)}, bf16[2,256,128]{2,1,0:T(8,128)(2,1)S(1)}, u32[]{:S(2)}, u32[]{:S(2)}) collective-permute-start(bf16[2,256,128]{2,1,0:T(8,128)(2,1)S(1)} %get-tuple-element.18), channel_id=1, source_target_pairs={{0,1},{1,0},{2,3},{3,2},{4,5},{5,4},{6,7},{7,6},{8,9},{9,8},{10,11... | collective-permute-start | bytes 393224 | tf_op jit(solution)/shard_map/ppermute | solution.py:212
  7.4 0.1 collective-permute-start.3
  7.5 0.4 %collective-permute-start.2 = (bf16[2,256,128]{2,1,0:T(8,128)(2,1)S(1)}, bf16[2,256,128]{2,1,0:T(8,128)(2,1)S(1)}, u32[]{:S(2)}, u32[]{:S(2)}) collective-permute-start(bf16[2,256,128]{2,1,0:T(8,128)(2,1)S(1)} %get-tuple-element.19), channel_id=1, source_target_pairs={{0,1},{1,0},{2,3},{3,2},{4,5},{5,4},{6,7},{7,6},{8,9},{9,8},{10,11... | collective-permute-start | bytes 393224 | tf_op jit(solution)/shard_map/ppermute | solution.py:212
  7.9 0.5 %collective-permute-done = bf16[2,256,128]{2,1,0:T(8,128)(2,1)S(1)} collective-permute-done((bf16[2,256,128]{2,1,0:T(8,128)(2,1)S(1)}, bf16[2,256,128]{2,1,0:T(8,128)(2,1)S(1)}, u32[]{:S(2)}, u32[]{:S(2)}) %collective-permute-start) | collective-permute-done | bytes 131104 | tf_op jit(solution)/shard_map/ppermute | solution.py:212
  8.4 0.5 %collective-permute-start.1 = (bf16[2,256,128]{2,1,0:T(8,128)(2,1)S(1)}, bf16[2,256,128]{2,1,0:T(8,128)(2,1)S(1)}, u32[]{:S(2)}, u32[]{:S(2)}) collective-permute-start(bf16[2,256,128]{2,1,0:T(8,128)(2,1)S(1)} %add_convert_fusion.1), channel_id=1, source_target_pairs={{0,3},{1,2},{2,1},{3,0},{4,7},{5,6},{6,5},{7,4},{8,11},{9,10},{10,... | collective-permute-start | bytes 393224 | tf_op jit(solution)/shard_map/ppermute | solution.py:212
  8.9 0.0 collective-permute-done.3
  9.0 4.2 %collective-permute-start.4 = (bf16[2,256,128]{2,1,0:T(8,128)(2,1)S(1)}, bf16[2,256,128]{2,1,0:T(8,128)(2,1)S(1)}, u32[]{:S(2)}, u32[]{:S(2)}) collective-permute-start(bf16[2,256,128]{2,1,0:T(8,128)(2,1)S(1)} %add_convert_fusion), channel_id=1, source_target_pairs={{2,4},{3,5},{4,2},{5,3},{6,8},{7,9},{8,6},{9,7},{10,12},{11,13},{1... | collective-permute-start | bytes 393224 | tf_op jit(solution)/shard_map/ppermute | solution.py:212
  13.1 3.3 %collective-permute-start.5 = (bf16[256,128]{1,0:T(8,128)(2,1)S(1)}, bf16[256,128]{1,0:T(8,128)(2,1)S(1)}, u32[]{:S(2)}, u32[]{:S(2)}) collective-permute-start(bf16[256,128]{1,0:T(8,128)(2,1)S(1)} %get-tuple-element.22), channel_id=1, source_target_pairs={{1,4},{3,6},{4,1},{5,8},{6,3},{7,10},{8,5},{9,12},{10,7},{11,14},{... | collective-permute-start | bytes 196616 | tf_op jit(solution)/shard_map/ppermute | solution.py:212
  16.5 0.0 copy-done
  16.5 0.3 %shard_map.57.matrix_ref = bf16[128,96]{1,0:T(8,128)(2,1)S(1)} custom-call(f32[2,16,64]{2,1,0:T(8,128)S(1)} %bitcast.4), custom_call_target="tpu_custom_call" | custom-call | flops 10000000 | bytes 32768 | tf_op jit(solution)/shard_map/pallas_call | solution.py:250
  16.8 0.0 collective-permute-done.1.near_ref
  16.8 0.7 %shard_map.56.own_ref = f32[2,256,128]{2,1,0:T(8,128)S(1)} custom-call(bf16[8,2,16,2048]{3,2,1,0:T(8,128)(2,1)S(1)} %get-tuple-element.14.rows, bf16[2,2048,256]{2,1,0:T(8,128)(2,1)S(1)} %get-tuple-element.15.centre, f32[2,256,128]{2,1,0:T(8,128)S(1)} %get-tuple-element.16.own_ref, bf16[2,256,128]{2,1,0:T(8,128)(2,1)S(1)} %collective-permute-done.1.near_ref), custom_call_target="tpu_custom_call" | custom-call | flops 536870912 | bytes 1048576 | tf_op jit(solution)/shard_map/pallas_call | solution.py:259
  17.5 1.2 %collective-permute-done.5.far_ref = bf16[256,128]{1,0:T(8,128)(2,1)S(1)} collective-permute-done((bf16[256,128]{1,0:T(8,128)(2,1)S(1)}, bf16[256,128]{1,0:T(8,128)(2,1)S(1)}, u32[]{:S(2)}, u32[]{:S(2)}) %collective-permute-start.5) | collective-permute-done | bytes 65568 | tf_op jit(solution)/shard_map/ppermute | solution.py:212
  18.8 0.0 collective-permute-done.2.mid_ref
  18.8 0.0 collective-permute-done.4.next_ref
  18.8 1.3 %shard_map.58 = f32[128,8,256]{2,1,0:T(8,128)} custom-call(f32[2,256,128]{2,1,0:T(8,128)S(1)} %shard_map.56.own_ref, bf16[2,256,128]{2,1,0:T(8,128)(2,1)S(1)} %collective-permute-done.2.mid_ref, bf16[2,256,128]{2,1,0:T(8,128)(2,1)S(1)} %collective-permute-done.4.next_ref, bf16[256,128]{1,0:T(8,128)(2,1)S(1)} %collective-permute-done.5.far_ref, ...), custom_call_target="tpu_custom_call" | custom-call | flops 100000000 | bytes 2097152 | tf_op jit(solution)/shard_map/pallas_call | solution.py:268
  (2 shorter events, 0.1 us)
Async XLA Ops:
  0.0 16.5 %copy-start = (f32[2,64,16]{1,2,0:T(8,128)S(1)}, f32[2,64,16]{1,2,0:T(8,128)}, u32[]{:S(2)}) copy-start(f32[2,64,16]{1,2,0:T(8,128)} %param.7) | copy-start | bytes 24580
  6.6 1.8 %collective-permute-start = (bf16[2,256,128]{2,1,0:T(8,128)(2,1)S(1)}, bf16[2,256,128]{2,1,0:T(8,128)(2,1)S(1)}, u32[]{:S(2)}, u32[]{:S(2)}) collective-permute-start(bf16[2,256,128]{2,1,0:T(8,128)(2,1)S(1)} %get-tuple-element.18), channel_id=1, source_target_pairs={{0,1},{1,0},{2,3},{3,2},{4,5},{5,4},{6,7},{7,6},{8,9},{9,8},{10,11... | collective-permute-start | bytes 393224 | tf_op jit(solution)/shard_map/ppermute | solution.py:212
  7.4 1.5 %collective-permute-start.3 = (bf16[2,256,128]{2,1,0:T(8,128)(2,1)S(1)}, bf16[2,256,128]{2,1,0:T(8,128)(2,1)S(1)}, u32[]{:S(2)}, u32[]{:S(2)}) collective-permute-start(bf16[2,256,128]{2,1,0:T(8,128)(2,1)S(1)} %get-tuple-element.21), channel_id=1, source_target_pairs={{0,1},{1,0},{2,3},{3,2},{4,5},{5,4},{6,7},{7,6},{8,9},{9,8},{10,11... | collective-permute-start | bytes 393224 | tf_op jit(solution)/shard_map/ppermute | solution.py:212
  7.5 11.3 %collective-permute-start.2 = (bf16[2,256,128]{2,1,0:T(8,128)(2,1)S(1)}, bf16[2,256,128]{2,1,0:T(8,128)(2,1)S(1)}, u32[]{:S(2)}, u32[]{:S(2)}) collective-permute-start(bf16[2,256,128]{2,1,0:T(8,128)(2,1)S(1)} %get-tuple-element.19), channel_id=1, source_target_pairs={{0,1},{1,0},{2,3},{3,2},{4,5},{5,4},{6,7},{7,6},{8,9},{9,8},{10,11... | collective-permute-start | bytes 393224 | tf_op jit(solution)/shard_map/ppermute | solution.py:212
  8.4 8.4 %collective-permute-start.1 = (bf16[2,256,128]{2,1,0:T(8,128)(2,1)S(1)}, bf16[2,256,128]{2,1,0:T(8,128)(2,1)S(1)}, u32[]{:S(2)}, u32[]{:S(2)}) collective-permute-start(bf16[2,256,128]{2,1,0:T(8,128)(2,1)S(1)} %add_convert_fusion.1), channel_id=1, source_target_pairs={{0,3},{1,2},{2,1},{3,0},{4,7},{5,6},{6,5},{7,4},{8,11},{9,10},{10,... | collective-permute-start | bytes 393224 | tf_op jit(solution)/shard_map/ppermute | solution.py:212
  9.0 9.8 %collective-permute-start.4 = (bf16[2,256,128]{2,1,0:T(8,128)(2,1)S(1)}, bf16[2,256,128]{2,1,0:T(8,128)(2,1)S(1)}, u32[]{:S(2)}, u32[]{:S(2)}) collective-permute-start(bf16[2,256,128]{2,1,0:T(8,128)(2,1)S(1)} %add_convert_fusion), channel_id=1, source_target_pairs={{2,4},{3,5},{4,2},{5,3},{6,8},{7,9},{8,6},{9,7},{10,12},{11,13},{1... | collective-permute-start | bytes 393224 | tf_op jit(solution)/shard_map/ppermute | solution.py:212
  13.1 5.6 %collective-permute-start.5 = (bf16[256,128]{1,0:T(8,128)(2,1)S(1)}, bf16[256,128]{1,0:T(8,128)(2,1)S(1)}, u32[]{:S(2)}, u32[]{:S(2)}) collective-permute-start(bf16[256,128]{1,0:T(8,128)(2,1)S(1)} %get-tuple-element.22), channel_id=1, source_target_pairs={{1,4},{3,6},{4,1},{5,8},{6,3},{7,10},{8,5},{9,12},{10,7},{11,14},{... | collective-permute-start | bytes 196616 | tf_op jit(solution)/shard_map/ppermute | solution.py:212
